TPU v7x, 512 devices: a whole 4x4x16 slice. The times are simulated.
512 devices in a mesh: space: 64 (over y_hi, z, core), snap: 8 (over x, y_lo).
Axes of the slice: x: 4, y: 4 (y_hi: 2, y_lo: 2; y = y_hi * 2 + y_lo), z: 16, core: 2. Of those that a mesh axis runs over, the one named last changes fastest.
Arguments:
- snaps_primal: bfloat16 [2048, 196608], P('snap', 'space'), may hold values from -6 to 6
- snaps_adjoint: bfloat16 [2048, 196608], P('snap', 'space'), may hold values from -6 to 6
- coef_primal: bfloat16 [2048, 256], P('snap'), may hold values from -0.1875 to 0.1875
- coef_adjoint: bfloat16 [2048, 256], P('snap'), may hold values from -0.1875 to 0.1875
- op_blocks: bfloat16 [1536, 5, 128, 128], P('space'), may hold values from -0.25 to 0.25
- counts: int32 [1536], P('space'), may hold values from 1 to 5, as said below
- col_index: int32 [1536, 5], P('space'), may hold values from 0 to 47, as said below
- ghost_send: int32 [64, 4, 6], P('space'), may hold values from 0 to 23, as said below
Outputs:
- primal_modes: bfloat16 [256, 196608], P('snap', 'space')
- applied: bfloat16 [256, 196608], P('snap', 'space')
- reduced_operator: float32 [256, 256], P(None, 'snap')
- cross_gram: float32 [256, 256], P(None, 'snap')
Inputs may be any that keep to these rules, and one draw needn't show every extreme that they name: `counts`: every block row has its slot 0 live. `col_index`: slot 0 of every block row names the row's own diagonal block; ghost entries never name a partition outside 0 to 63. `ghost_send`: the 6 entries of one list are distinct.
All inputs are finite; a program needn't handle non-finite values.
Results may differ from a plain program's by a relative error of at most 0.02.
Values may be sent and summed in bfloat16 or wider, within the bound.
No kernel may reach another device: no remote copies, remote signals or barrier semaphores. Data moves between devices by JAX's collectives and lax.ppermute only.
A program may use at most 64 MiB of HBM per device.

v0:
```python
import math

import jax
import jax.numpy as jnp
from jax import lax
from jax.sharding import PartitionSpec as P


def in_blocks(array, dim, count):
    before, after = (array.shape[:dim], array.shape[dim + 1 :])
    return jnp.moveaxis(array.reshape(*before, count, -1, *after), dim, 0)


def summed_on_arrival(array, axis, dim):
    count = lax.axis_size(axis)
    tiles = lax.all_to_all(in_blocks(array, dim, count), axis, 0, 0, tiled=True)
    return jnp.sum(tiles.astype(jnp.float32), axis=0)


def passed_along(value, axis, steps):
    count = lax.axis_size(axis)
    first, last = (max(0, -steps), min(count, count - steps))
    return lax.ppermute(value, axis, [(source, source + steps) for source in range(first, last)])


def laid_out(tiles, dim):
    tiles = jnp.moveaxis(tiles, 0, dim)
    lengths = tiles.shape
    return tiles.reshape(*lengths[:dim], lengths[dim] * lengths[dim + 1], *lengths[dim + 2 :])


def from_everyone(array, axis):
    count = lax.axis_size(axis)
    return lax.all_to_all(
        jnp.broadcast_to(array[None], (count, *array.shape)), axis, 0, 0, tiled=True
    )


def collect(array, axis, dim):
    return laid_out(from_everyone(array, axis), dim)


def filled_up(lines, count):
    spare = -lines.shape[0] % count
    if not spare:
        return lines
    return jnp.concatenate([lines, jnp.zeros((spare, *lines.shape[1:]), lines.dtype)])


def summed_on_arrival_2(array, axis, dim):
    tiles = in_blocks(array, dim, lax.axis_size(axis))
    arrived = lax.all_to_all(tiles, axis, split_axis=0, concat_axis=0, tiled=True)
    return arrived.sum(axis=0)


def total_of(array, axes):
    padded = filled_up(array, lax.axis_size(axes))
    whole = collect(summed_on_arrival_2(padded, axes, 0), axes, 0)
    return lax.slice_in_dim(whole, 0, len(array)).reshape(array.shape)


def packed_total(arrays, axis):
    line, at, done = (jnp.concatenate([a.reshape(-1) for a in arrays]), 0, [])
    so_far = total_of(line, axis)
    for a in arrays:
        done.append(so_far[at : at + a.size].reshape(a.shape))
        at += a.size
    return tuple(done)


def project(coef, snaps):
    return jnp.einsum("mr,ms->rs", coef, snaps, preferred_element_type=jnp.float32)


def per_device(
    snaps_primal, snaps_adjoint, coef_primal, coef_adjoint, op_blocks, counts, col_index, ghost_send
):
    share = coef_primal.shape[1] // lax.axis_size("snap")
    unknowns = snaps_primal.shape[1]
    row_count = col_index.shape[0]
    slot_count = col_index.shape[1]
    block_size = op_blocks.shape[2]
    list_len = ghost_send.shape[2]
    both_shares = summed_on_arrival(
        jnp.concatenate(
            [project(coef_primal, snaps_primal), project(coef_adjoint, snaps_adjoint)], axis=1
        ).astype(jnp.bfloat16),
        "snap",
        0,
    ).astype(jnp.bfloat16)
    primal_share = both_shares[:, :unknowns]
    adjoint_share = both_shares[:, unknowns:]
    blocks = primal_share.reshape(share, row_count, block_size)
    outgoing = jnp.take(blocks, ghost_send[0], axis=1)
    from_far_low = passed_along(outgoing[:, 0], "space", 2)
    from_near_low = passed_along(outgoing[:, 1], "space", 1)
    from_near_high = passed_along(outgoing[:, 2], "space", -1)
    from_far_high = passed_along(outgoing[:, 3], "space", -2)
    received = jnp.stack([from_far_low, from_near_low, from_near_high, from_far_high], axis=1)
    extended = jnp.concatenate([blocks, received.reshape(share, 4 * list_len, block_size)], axis=1)
    picked = jnp.take(extended, col_index, axis=1)
    live = (jnp.arange(slot_count, dtype=jnp.int32)[None, :] < counts[:, None]).astype(jnp.bfloat16)
    picked = picked * live[None, :, :, None]
    applied = jnp.einsum("mrkc,rkjc->mrj", picked, op_blocks, preferred_element_type=jnp.float32)
    applied = applied.astype(jnp.bfloat16).reshape(share, unknowns)
    stacked = jnp.concatenate([applied, primal_share], axis=0)
    products = jnp.einsum(
        "as,bs->ab", collect(adjoint_share, "snap", 0), stacked, preferred_element_type=jnp.float32
    )
    factor = 1.0 / math.sqrt(unknowns * lax.axis_size("space"))
    reduced, gram = packed_total((products[:, :share], products[:, share:]), "space")
    return (primal_share, applied, reduced * factor, gram * factor)


def solution(mesh):
    placed = (
        P("snap", "space"),
        P("snap", "space"),
        P("snap", None),
        P("snap", None),
        P("space", None, None, None),
        P("space"),
        P("space", None),
        P("space", None, None),
    )
    return jax.shard_map(
        per_device,
        mesh=mesh,
        in_specs=placed,
        out_specs=(P("snap", "space"), P("snap", "space"), P(None, "snap"), P(None, "snap")),
        check_vma=False,
    )
```

profile of v0, /device:TPU:1, one launch (start us, length us, event | category | flops | bytes accessed | tf_op | source)
XLA Modules:
  0.0 147.3 jit_solution(8130733153580535770)
XLA Ops:
  0.7 1.4 copy-done
  2.0 1.5 %convolution_convert_fusion.1 = bf16[256,3072]{1,0:T(8,128)(2,1)S(1)} fusion(bf16[256,256]{1,0:T(8,128)(2,1)} %param.10, bf16[256,3072]{1,0:T(8,128)(2,1)S(1)} %copy-done), kind=kOutput, calls=%fused_computation.3 | convolution fusion | flops 403439616 | bytes 3276800 | tf_op jit(solution)/shard_map/mr,ms->rs/dot_general | solution.py:72
  3.6 0.6 convolution_convert_fusion
  4.2 2.0 %pad_maximum_fusion = bf16[8,32,6144]{2,1,0:T(8,128)(2,1)} fusion(bf16[8,32,3072]{2,1,0:T(8,128)(2,1)S(1)} %bitcast.58, bf16[8,32,3072]{2,1,0:T(8,128)(2,1)S(1)} %bitcast.57), kind=kLoop, calls=%fused_computation.4 | loop fusion | flops 6291456 | bytes 6291456 | tf_op jit(solution)/shard_map/concatenate | solution.py:85
  6.1 6.0 %all-to-all-start = ((bf16[8,32,6144]{2,1,0:T(8,128)(2,1)}), bf16[8,32,6144]{2,1,0:T(8,128)(2,1)}, u32[]{:S(2)}, u32[]{:S(2)}) async-start(bf16[8,32,6144]{2,1,0:T(8,128)(2,1)} %pad_maximum_fusion), calls=%async_computation | async-start | bytes 6291456 | tf_op jit(solution)/shard_map/all_to_all | solution.py:16
  12.5 40.5 %all-to-all-done = bf16[8,32,6144]{2,1,0:T(8,128)(2,1)} async-done(((bf16[8,32,6144]{2,1,0:T(8,128)(2,1)}), bf16[8,32,6144]{2,1,0:T(8,128)(2,1)}, u32[]{:S(2)}, u32[]{:S(2)}) %all-to-all-start) | async-done | bytes 3145760 | tf_op jit(solution)/shard_map/all_to_all | solution.py:16
  53.1 2.4 %reduce_sum.21 = bf16[32,6144]{1,0:T(8,128)(2,1)S(1)} reduce(bf16[8,32,6144]{2,1,0:T(8,128)(2,1)} %all-to-all-done, bf16[]{:T(256)} %constant.19.clone.1), dimensions={0}, to_apply=%region_0.0 | reduce | flops 1376256 | bytes 3538946 | tf_op jit(solution)/shard_map/reduce_sum | solution.py:17
  55.5 1.3 broadcast_in_dim.42
  56.9 4.3 %all-to-all-start.1 = ((bf16[8,32,3072]{2,1,0:T(8,128)(2,1)}), bf16[8,32,3072]{2,1,0:T(8,128)(2,1)}, u32[]{:S(2)}, u32[]{:S(2)}) async-start(bf16[8,32,3072]{2,1,0:T(8,128)(2,1)} %broadcast_in_dim.42), calls=%async_computation.1 | async-start | bytes 3145728 | tf_op jit(solution)/shard_map/all_to_all | solution.py:34
  61.2 0.6 gather_fusion
  61.9 5.4 %collective-permute-start.2 = (bf16[32,6,128]{2,0,1:T(8,128)(2,1)S(1)}, bf16[32,6,128]{2,0,1:T(8,128)(2,1)S(1)}, u32[]{:S(2)}, u32[]{:S(2)}) collective-permute-start(bf16[32,6,128]{2,0,1:T(8,128)(2,1)S(1)} %get-tuple-element.22), channel_id=1, source_target_pairs={{8,0},{16,8},{24,16},{32,24},{40,32},{48,40},{56,48},{64,56},{72,6... | collective-permute-start | bytes 147464 | tf_op jit(solution)/shard_map/ppermute | solution.py:23
  67.3 1.3 collective-permute-start.3
  68.6 6.3 %collective-permute-start = (bf16[32,6,128]{2,0,1:T(8,128)(2,1)S(1)}, bf16[32,6,128]{2,0,1:T(8,128)(2,1)S(1)}, u32[]{:S(2)}, u32[]{:S(2)}) collective-permute-start(bf16[32,6,128]{2,0,1:T(8,128)(2,1)S(1)} %get-tuple-element.20), channel_id=1, source_target_pairs={{0,16},{8,24},{16,32},{24,40},{32,48},{40,56},{48,64},{56,72},{64,... | collective-permute-start | bytes 147464 | tf_op jit(solution)/shard_map/ppermute | solution.py:23
  74.9 3.8 %collective-permute-start.1 = (bf16[32,6,128]{2,0,1:T(8,128)(2,1)S(1)}, bf16[32,6,128]{2,0,1:T(8,128)(2,1)S(1)}, u32[]{:S(2)}, u32[]{:S(2)}) collective-permute-start(bf16[32,6,128]{2,0,1:T(8,128)(2,1)S(1)} %get-tuple-element.23), channel_id=1, source_target_pairs={{0,8},{8,16},{16,24},{24,32},{32,40},{40,48},{48,56},{56,64},{64,7... | collective-permute-start | bytes 147464 | tf_op jit(solution)/shard_map/ppermute | solution.py:23
  78.7 0.1 copy.35
  78.8 1.0 collective-permute-done.1
  79.9 0.8 gather_fusion.1
  80.7 3.6 %fusion.1 = bf16[24,4,8,128]{3,2,1,0:T(8,128)(2,1)S(1)} fusion(bf16[24,5,128,128]{3,2,1,0:T(8,128)(2,1)} %param.12, bf16[24,5,32,128]{3,2,1,0:T(8,128)(2,1)S(1)} %bitcast.59, pred[24,5]{1,0:T(8,128)(4,1)S(1)} %copy.35, bf16[24,5]{1,0:T(8,128)(2,1)S(1)} %fusion.14), kind=kOutput, calls=%fused_computation.7 | convolution fusion | flops 126910464 | bytes 5112168 | tf_op jit(solution)/shard_map/mrkc,rkjc->mrj/dot_general | solution.py:104
  84.4 2.1 %fusion.8 = f32[256,64]{0,1:T(8,128)S(1)} fusion(bf16[256,3072]{1,0:T(8,128)(2,1)} %bitcast.20, bf16[32,3072]{1,0:T(8,128)(2,1)S(1)} %get-tuple-element.19, bf16[32,3072]{1,0:T(8,128)(2,1)S(1)} %bitcast.62), kind=kOutput, calls=%fused_computation.15 | convolution fusion | flops 101449728 | bytes 2031616 | tf_op jit(solution)/shard_map/as,bs->ab/dot_general | solution.py:107
  86.9 38.6 %all_to_all.25 = f32[64,1,256]{2,1,0:T(1,128)S(1)} all-to-all(f32[64,1,256]{2,1,0:T(1,128)S(1)} %copy.42), channel_id=1, replica_groups=mesh['space'=64,'snap'=8] {'space'}, dimensions={0} | all-to-all | bytes 131072 | tf_op jit(solution)/shard_map/all_to_all | solution.py:52
  125.7 19.8 %all_to_all.26 = f32[64,1,256]{2,1,0:T(1,128)S(1)} all-to-all(f32[64,1,256]{2,1,0:T(1,128)S(1)} %broadcast_in_dim.43), channel_id=1, replica_groups=mesh['space'=64,'snap'=8] {'space'}, dimensions={0} | all-to-all | bytes 131072 | tf_op jit(solution)/shard_map/all_to_all | solution.py:34
  145.5 0.2 fusion.12
  145.8 0.7 copy.43
  146.6 0.7 copy.44
  (47 shorter events, 1.5 us)
Async XLA Ops:
  0.6 1.4 copy-start
  0.6 2.9 %copy-start.4 = (bf16[256,256]{1,0:T(8,128)(2,1)S(1)}, bf16[256,256]{1,0:T(8,128)(2,1)}, u32[]{:S(2)}) copy-start(bf16[256,256]{1,0:T(8,128)(2,1)} %param.11) | copy-start | bytes 393220
  0.7 2.9 %copy-start.1 = (bf16[256,3072]{1,0:T(8,128)(2,1)S(1)}, bf16[256,3072]{1,0:T(8,128)(2,1)}, u32[]{:S(2)}) copy-start(bf16[256,3072]{1,0:T(8,128)(2,1)} %param.9) | copy-start | bytes 4718596
  6.1 6.0 %copy-start.6 = (s32[1,4,6]{2,1,0:T(4,128)S(1)}, s32[1,4,6]{2,1,0:T(4,128)}, u32[]{:S(2)}) copy-start(s32[1,4,6]{2,1,0:T(4,128)} %param.15) | copy-start | bytes 292
  6.1 6.1 %copy-start.5 = (s32[24,5]{0,1:T(8,128)S(1)}, s32[24,5]{0,1:T(8,128)}, u32[]{:S(2)}) copy-start(s32[24,5]{0,1:T(8,128)} %param.14) | copy-start | bytes 1444
  6.1 6.3 %copy-start.7 = (s32[24]{0:T(128)S(1)}, s32[24]{0:T(128)}, u32[]{:S(2)}) copy-start(s32[24]{0:T(128)} %param.13) | copy-start | bytes 292
  6.1 47.0 %all-to-all-start = ((bf16[8,32,6144]{2,1,0:T(8,128)(2,1)}), bf16[8,32,6144]{2,1,0:T(8,128)(2,1)}, u32[]{:S(2)}, u32[]{:S(2)}) async-start(bf16[8,32,6144]{2,1,0:T(8,128)(2,1)} %pad_maximum_fusion), calls=%async_computation | async-start | bytes 6291456 | tf_op jit(solution)/shard_map/all_to_all | solution.py:16
  55.5 28.9 %copy-start.2 = (bf16[32,3072]{1,0:T(8,128)(2,1)}, bf16[32,3072]{1,0:T(8,128)(2,1)S(1)}, u32[]{:S(2)}) copy-start(bf16[32,3072]{1,0:T(8,128)(2,1)S(1)} %get-tuple-element.19) | copy-start | bytes 589828
  56.9 27.5 %all-to-all-start.1 = ((bf16[8,32,3072]{2,1,0:T(8,128)(2,1)}), bf16[8,32,3072]{2,1,0:T(8,128)(2,1)}, u32[]{:S(2)}, u32[]{:S(2)}) async-start(bf16[8,32,3072]{2,1,0:T(8,128)(2,1)} %broadcast_in_dim.42), calls=%async_computation.1 | async-start | bytes 3145728 | tf_op jit(solution)/shard_map/all_to_all | solution.py:34
  61.9 16.9 %collective-permute-start.2 = (bf16[32,6,128]{2,0,1:T(8,128)(2,1)S(1)}, bf16[32,6,128]{2,0,1:T(8,128)(2,1)S(1)}, u32[]{:S(2)}, u32[]{:S(2)}) collective-permute-start(bf16[32,6,128]{2,0,1:T(8,128)(2,1)S(1)} %get-tuple-element.22), channel_id=1, source_target_pairs={{8,0},{16,8},{24,16},{32,24},{40,32},{48,40},{56,48},{64,56},{72,6... | collective-permute-start | bytes 147464 | tf_op jit(solution)/shard_map/ppermute | solution.py:23
  67.3 11.5 %collective-permute-start.3 = (bf16[32,6,128]{2,0,1:T(8,128)(2,1)S(1)}, bf16[32,6,128]{2,0,1:T(8,128)(2,1)S(1)}, u32[]{:S(2)}, u32[]{:S(2)}) collective-permute-start(bf16[32,6,128]{2,0,1:T(8,128)(2,1)S(1)} %get-tuple-element.21), channel_id=1, source_target_pairs={{16,0},{24,8},{32,16},{40,24},{48,32},{56,40},{64,48},{72,56},{80,... | collective-permute-start | bytes 147464 | tf_op jit(solution)/shard_map/ppermute | solution.py:23
  68.6 10.2 %collective-permute-start = (bf16[32,6,128]{2,0,1:T(8,128)(2,1)S(1)}, bf16[32,6,128]{2,0,1:T(8,128)(2,1)S(1)}, u32[]{:S(2)}, u32[]{:S(2)}) collective-permute-start(bf16[32,6,128]{2,0,1:T(8,128)(2,1)S(1)} %get-tuple-element.20), channel_id=1, source_target_pairs={{0,16},{8,24},{16,32},{24,40},{32,48},{40,56},{48,64},{56,72},{64,... | collective-permute-start | bytes 147464 | tf_op jit(solution)/shard_map/ppermute | solution.py:23
  74.9 5.0 %collective-permute-start.1 = (bf16[32,6,128]{2,0,1:T(8,128)(2,1)S(1)}, bf16[32,6,128]{2,0,1:T(8,128)(2,1)S(1)}, u32[]{:S(2)}, u32[]{:S(2)}) collective-permute-start(bf16[32,6,128]{2,0,1:T(8,128)(2,1)S(1)} %get-tuple-element.23), channel_id=1, source_target_pairs={{0,8},{8,16},{16,24},{24,32},{32,40},{40,48},{48,56},{56,64},{64,7... | collective-permute-start | bytes 147464 | tf_op jit(solution)/shard_map/ppermute | solution.py:23
  84.3 41.2 %copy-start.3 = (bf16[24,4,8,128]{3,2,0,1:T(8,128)(2,1)}, bf16[24,4,8,128]{3,2,0,1:T(8,128)(2,1)S(1)}, u32[]{:S(2)}) copy-start(bf16[24,4,8,128]{3,2,0,1:T(8,128)(2,1)S(1)} %copy.50) | copy-start | bytes 589828
where the time goes:
time: 148 us; the launch traced here: 147 us
  blocking collectives  58.5 us (40%)
  waiting for transfers between devices  41.6 us (28%)
  starting transfers between devices  27 us (18%)
  matrix products  7.73 us (5%)
  local copies, waits for them, and re-layouts  6.66 us (4%)
  other arithmetic  4.89 us (3%)
    all_to_all x1, waiting for transfers between devices, summed_on_arrival(): tiles = lax.all_to_all(in_blocks(array, dim, count), axis, 0, 0, tiled=True)  40.5 us
    all_to_all x1, blocking collectives, summed_on_arrival_2(): lax.all_to_all(tiles, axis, split_axis=0, concat_axis=0, tiled=True)  38.6 us
    all_to_all x1, blocking collectives, from_everyone(): lax.all_to_all(jnp.broadcast_to(array[None], (count, *array.shape)), axis...  19.8 us
    ppermute x4, starting transfers between devices, passed_along(): lax.ppermute(value, axis, [(source, source + steps) for source in range(f...  16.8 us
    all_to_all x1, starting transfers between devices, summed_on_arrival(): tiles = lax.all_to_all(in_blocks(array, dim, count), axis, 0, 0, tiled=True)  5.99 us
    all_to_all x1, starting transfers between devices, from_everyone(): lax.all_to_all(jnp.broadcast_to(array[None], (count, *array.shape)), axis...  4.28 us
    dot_general x1, matrix products, per_device(): jnp.einsum('mrkc,rkjc->mrj', picked, op_blocks, preferred_element_type=jn...  3.58 us
  transfers between devices with their start and end apart: 6, of which 2 were waited for; matrix products, arithmetic and copies ran while one was open for 4% of the time, Pallas kernels for 0%

commit v1 on v0

v1 whole, which is shorter than its diff:
```python
import math

import jax
import jax.numpy as jnp
from jax import lax
from jax.sharding import PartitionSpec as P

F32 = jnp.float32
BF16 = jnp.bfloat16


def exchange(tiles, axis, groups=None):
    return lax.all_to_all(tiles, axis, 0, 0, tiled=True, axis_index_groups=groups)


def passed_along(value, axis, steps):
    count = lax.axis_size(axis)
    first, last = (max(0, -steps), min(count, count - steps))
    return lax.ppermute(value, axis, [(source, source + steps) for source in range(first, last)])


def space_groups(count):
    far, half = count // 8, count // 2
    near_of = [[h * half + f * 4 + low for h in range(2) for low in range(4)] for f in range(far)]
    far_of = [[h * half + f * 4 + low for f in range(far)] for h in range(2) for low in range(4)]
    return near_of, far_of


def total_over_space(terms):
    near, far = space_groups(lax.axis_size("space"))
    rows, cols = terms.shape
    mine = exchange(terms.reshape(8, rows // 8, cols), "space", near).sum(axis=0)
    every = exchange(jnp.broadcast_to(mine[None], (len(far[0]), *mine.shape)), "space", far)
    mine = every.sum(axis=0)
    return exchange(jnp.broadcast_to(mine[None], (8, *mine.shape)), "space", near).reshape(rows, cols)


def per_device(
    snaps_primal, snaps_adjoint, coef_primal, coef_adjoint, op_blocks, counts, col_index, ghost_send
):
    ways = lax.axis_size("snap")
    modes = coef_primal.shape[1]
    share = modes // ways
    unknowns = snaps_primal.shape[1]
    piece = unknowns // ways
    row_count, slot_count = col_index.shape
    block_size = op_blocks.shape[2]
    list_len = ghost_send.shape[2]

    primal_part = jnp.einsum("mr,ms->rs", coef_primal, snaps_primal, preferred_element_type=F32)
    primal_tiles = exchange(primal_part.astype(BF16).reshape(ways, share, unknowns), "snap")
    adjoint_part = jnp.einsum(
        "mr,mws->wrs",
        coef_adjoint,
        snaps_adjoint.reshape(-1, ways, piece),
        preferred_element_type=F32,
    )
    adjoint_tiles = exchange(adjoint_part.astype(BF16), "snap")
    primal = primal_tiles.astype(F32).sum(axis=0).astype(BF16)

    blocks = primal.reshape(share, row_count, block_size)
    outgoing = jnp.take(blocks, ghost_send[0], axis=1)
    received = jnp.stack(
        [passed_along(outgoing[:, d], "space", step) for d, step in enumerate((2, 1, -1, -2))], axis=1
    )
    extended = jnp.concatenate([blocks, received.reshape(share, 4 * list_len, block_size)], axis=1)
    picked = jnp.take(extended, col_index, axis=1)
    live = (jnp.arange(slot_count, dtype=jnp.int32)[None, :] < counts[:, None]).astype(BF16)
    picked = picked * live[None, :, :, None]
    applied = jnp.einsum("mrkc,rkjc->mrj", picked, op_blocks, preferred_element_type=F32)
    applied = applied.astype(BF16).reshape(share, unknowns)

    both = jnp.stack([applied, primal]).reshape(2 * share, ways, piece)
    both = exchange(jnp.moveaxis(both, 1, 0), "snap")
    adjoint = adjoint_tiles.astype(F32).sum(axis=0).astype(BF16)
    products = jnp.einsum("was,bs->wab", both, adjoint, preferred_element_type=F32)
    mine = exchange(products.astype(BF16), "snap").astype(F32).sum(axis=0)
    total = total_over_space(mine) * (1.0 / math.sqrt(unknowns * lax.axis_size("space")))
    return (primal, applied, total[:share].T, total[share:].T)


def solution(mesh):
    placed = (
        P("snap", "space"),
        P("snap", "space"),
        P("snap", None),
        P("snap", None),
        P("space", None, None, None),
        P("space"),
        P("space", None),
        P("space", None, None),
    )
    return jax.shard_map(
        per_device,
        mesh=mesh,
        in_specs=placed,
        out_specs=(P("snap", "space"), P("snap", "space"), P(None, "snap"), P(None, "snap")),
        check_vma=False,
    )
```

time: 148 us -> 146 us (0.986)
  waiting for transfers between devices: 41.6 us -> 24 us
  starting transfers between devices: 27 us -> 37.9 us
  blocking collectives: 58.5 us -> 48.8 us
  local copies, waits for them, and re-layouts: 6.66 us -> 14.6 us
  matrix products: 7.73 us -> 10.9 us
  other arithmetic: 4.89 us -> 7.77 us
    all_to_all x2 -> x4, waiting for transfers between devices: 40.5 us -> 23.9 us  [exchange(): lax.all_to_all(tiles, axis, 0, 0, tiled=True, axis_index_groups=groups)]
    all_to_all x2 -> x4, starting transfers between devices: 10.3 us -> 21.5 us  [exchange(): lax.all_to_all(tiles, axis, 0, 0, tiled=True, axis_index_groups=groups)]
    all_to_all x2 -> x3, blocking collectives: 58.5 us -> 48.8 us  [exchange(): lax.all_to_all(tiles, axis, 0, 0, tiled=True, axis_index_groups=groups)]
    reshape x2 -> x4, local copies, waits for them, and re-layouts: 0.1 us -> 4.13 us  [the longest x1 2.61 us: per_device(): snaps_adjoint.reshape(-1, ways, piece)]
    dot_general x4, matrix products: 7.73 us -> 10.9 us  [the longest x1 3.91 us: per_device(): jnp.einsum('mrkc,rkjc->mrj', picked, op_blocks, preferred_element_type=F32)]
    concatenate x1 -> x0, other arithmetic: 1.96 us -> none  [per_device(): jnp.concatenate([project(coef_primal, snaps_primal), project(coef_adjoint...]
    another operation x1 -> x2, other arithmetic: 0.03 us -> 1.86 us  [the longest x1 0.96 us: per_device(): both = jnp.stack([applied, primal]).reshape(2 * share, ways, piece)]
    unnamed x18 -> x25, local copies, waits for them, and re-layouts: 2.82 us -> 3.35 us
  transfers between devices with their start and end apart: 6 -> 8, of which waited for: 2 -> 4; matrix products, arithmetic and copies ran while one was open for 4% -> 17% of each run, Pallas kernels for 0% -> 0%
where the time goes in v1:
time: 146 us; the launch traced here: 145 us
  blocking collectives  48.8 us (33%)
  starting transfers between devices  37.9 us (26%)
  waiting for transfers between devices  24 us (16%)
  local copies, waits for them, and re-layouts  14.6 us (10%)
  matrix products  10.9 us (7%)
  other arithmetic  7.77 us (5%)
    all_to_all x3, blocking collectives, exchange(): lax.all_to_all(tiles, axis, 0, 0, tiled=True, axis_index_groups=groups)  48.8 us
    all_to_all x4, waiting for transfers between devices, exchange(): lax.all_to_all(tiles, axis, 0, 0, tiled=True, axis_index_groups=groups)  23.9 us
    all_to_all x4, starting transfers between devices, exchange(): lax.all_to_all(tiles, axis, 0, 0, tiled=True, axis_index_groups=groups)  21.5 us
    ppermute x4, starting transfers between devices, passed_along(): lax.ppermute(value, axis, [(source, source + steps) for source in range(f...  16.4 us
    dot_general x1, matrix products, per_device(): jnp.einsum('mrkc,rkjc->mrj', picked, op_blocks, preferred_element_type=F32)  3.91 us
    unnamed x25, local copies, waits for them, and re-layouts  3.35 us
    dot_general x1, matrix products, per_device(): jnp.einsum('mr,mws->wrs', coef_adjoint, snaps_adjoint.reshape(-1, ways, p...  3.13 us
  transfers between devices with their start and end apart: 8, of which 4 were waited for; matrix products, arithmetic and copies ran while one was open for 17% of the time, Pallas kernels for 0%

profile of v1, /device:TPU:1, one launch (start us, length us, event | category | flops | bytes accessed | tf_op | source)
XLA Modules:
  0.0 144.9 jit_solution(13967984038846183845)
XLA Ops:
  0.6 1.4 copy-done
  2.0 2.7 %convolution_convert_fusion = bf16[256,3072]{1,0:T(8,128)(2,1)} fusion(bf16[256,256]{1,0:T(8,128)(2,1)} %param.10, bf16[256,3072]{1,0:T(8,128)(2,1)S(1)} %copy-done), kind=kOutput, calls=%fused_computation.2 | convolution fusion | flops 403439616 | bytes 3276800 | tf_op jit(solution)/shard_map/mr,ms->rs/dot_general | solution.py:50
  4.7 6.0 %all-to-all-start = ((bf16[8,32,3072]{2,1,0:T(8,128)(2,1)}), bf16[8,32,3072]{2,1,0:T(8,128)(2,1)S(1)}, u32[]{:S(2)}, u32[]{:S(2)}) async-start(bf16[8,32,3072]{2,1,0:T(8,128)(2,1)} %bitcast.75), calls=%async_computation | async-start | bytes 3145728 | tf_op jit(solution)/shard_map/all_to_all | solution.py:13
  11.5 2.6 %copy.52 = bf16[256,3072]{0,1:T(8,128)(2,1)} copy(bf16[256,3072]{1,0:T(8,128)(2,1)} %param.9) | data formatting | bytes 3145728 | tf_op jit(solution)/shard_map/reshape | solution.py:55
  14.7 3.1 %fusion = bf16[8,256,384]{1,2,0:T(8,128)(2,1)} fusion(bf16[256,8,384]{0,2,1:T(8,128)(2,1)} %bitcast.76, bf16[256,256]{1,0:T(8,128)(2,1)S(1)} %copy-done.7), kind=kOutput, calls=%fused_computation.4 | convolution fusion | flops 403439616 | bytes 3276800 | tf_op jit(solution)/shard_map/mr,mws->wrs/dot_general | solution.py:52
  17.9 12.0 %all-to-all-done = bf16[8,32,3072]{2,1,0:T(8,128)(2,1)S(1)} async-done(((bf16[8,32,3072]{2,1,0:T(8,128)(2,1)}), bf16[8,32,3072]{2,1,0:T(8,128)(2,1)S(1)}, u32[]{:S(2)}, u32[]{:S(2)}) %all-to-all-start) | async-done | bytes 1572896 | tf_op jit(solution)/shard_map/all_to_all | solution.py:13
  29.9 1.2 copy-done.1
  31.0 4.4 %all-to-all-start.2 = ((bf16[8,256,384]{1,2,0:T(8,128)(2,1)}), bf16[8,256,384]{1,2,0:T(8,128)(2,1)S(1)}, u32[]{:S(2)}, u32[]{:S(2)}) async-start(bf16[8,256,384]{1,2,0:T(8,128)(2,1)} %fusion), calls=%async_computation.2 | async-start | bytes 3145728 | tf_op jit(solution)/shard_map/all_to_all | solution.py:13
  35.5 1.7 %reduce_sum.51 = bf16[32,3072]{1,0:T(8,128)(2,1)S(1)} reduce(bf16[8,32,3072]{2,1,0:T(8,128)(2,1)} %copy-done.1, bf16[]{:T(256)} %constant.28.clone.1), dimensions={0}, to_apply=%region_0.0 | reduce | flops 688128 | bytes 1769474 | tf_op jit(solution)/shard_map/reduce_sum | solution.py:59
  37.2 1.3 gather_fusion
  40.2 7.2 %collective-permute-start = (bf16[32,6,128]{2,0,1:T(8,128)(2,1)}, bf16[32,6,128]{2,0,1:T(8,128)(2,1)}, u32[]{:S(2)}, u32[]{:S(2)}) collective-permute-start(bf16[32,6,128]{2,0,1:T(8,128)(2,1)} %get-tuple-element.4), channel_id=1, source_target_pairs={{0,16},{8,24},{16,32},{24,40},{32,48},{40,56},{48,64},{56,72},{64,... | collective-permute-start | bytes 147464 | tf_op jit(solution)/shard_map/ppermute | solution.py:19
  47.3 1.3 collective-permute-start.3
  48.6 3.8 %collective-permute-start.2 = (bf16[32,6,128]{2,0,1:T(8,128)(2,1)}, bf16[32,6,128]{2,0,1:T(8,128)(2,1)}, u32[]{:S(2)}, u32[]{:S(2)}) collective-permute-start(bf16[32,6,128]{2,0,1:T(8,128)(2,1)} %get-tuple-element.6), channel_id=1, source_target_pairs={{8,0},{16,8},{24,16},{32,24},{40,32},{48,40},{56,48},{64,56},{72,6... | collective-permute-start | bytes 147464 | tf_op jit(solution)/shard_map/ppermute | solution.py:19
  52.4 4.2 %collective-permute-start.1 = (bf16[32,6,128]{2,0,1:T(8,128)(2,1)}, bf16[32,6,128]{2,0,1:T(8,128)(2,1)}, u32[]{:S(2)}, u32[]{:S(2)}) collective-permute-start(bf16[32,6,128]{2,0,1:T(8,128)(2,1)} %get-tuple-element.7), channel_id=1, source_target_pairs={{0,8},{8,16},{16,24},{24,32},{32,40},{40,48},{48,56},{56,64},{64,7... | collective-permute-start | bytes 147464 | tf_op jit(solution)/shard_map/ppermute | solution.py:19
  60.0 1.7 %gather_fusion.1 = bf16[120,32,128]{2,1,0:T(8,128)(2,1)} fusion(bf16[32,48,128]{2,0,1:T(8,128)(2,1)S(1)} %pad_maximum_fusion, s32[1024]{0:T(1024)S(1)} %pad_clamp_fusion), kind=kCustom, calls=%fused_computation.1 | custom fusion | bytes 1966560 | tf_op jit(solution)/shard_map/jit(_take)/gather | solution.py:67
  61.6 3.9 %fusion.1 = bf16[24,32,128]{2,1,0:T(8,128)(2,1)S(1)} fusion(bf16[24,5,128,128]{3,2,1,0:T(8,128)(2,1)} %param.12, bf16[24,5,32,128]{3,2,1,0:T(8,128)(2,1)} %bitcast.77, pred[24,5]{1,0:T(8,128)(4,1)S(1)} %copy-done.10, bf16[24,5]{1,0:T(8,128)(2,1)S(1)} %fusion.10), kind=kOutput, calls=%fused_computation.7 | convolution fusion | flops 126910464 | bytes 5112168 | tf_op jit(solution)/shard_map/mrkc,rkjc->mrj/dot_general | solution.py:70
  68.9 5.3 %all-to-all-start.1 = ((bf16[8,64,384]{2,1,0:T(8,128)(2,1)}), bf16[8,64,384]{2,1,0:T(8,128)(2,1)S(1)}, u32[]{:S(2)}, u32[]{:S(2)}) async-start(bf16[8,64,384]{2,1,0:T(8,128)(2,1)} %bitcast.74), calls=%async_computation.1 | async-start | bytes 786432 | tf_op jit(solution)/shard_map/all_to_all | solution.py:13
  75.2 6.9 %all-to-all-done.1 = bf16[8,64,384]{2,1,0:T(8,128)(2,1)S(1)} async-done(((bf16[8,64,384]{2,1,0:T(8,128)(2,1)}), bf16[8,64,384]{2,1,0:T(8,128)(2,1)S(1)}, u32[]{:S(2)}, u32[]{:S(2)}) %all-to-all-start.1) | async-done | bytes 393248 | tf_op jit(solution)/shard_map/all_to_all | solution.py:13
  82.1 1.2 convolution_convert_fusion.2
  83.3 8.9 %all_to_all.35 = bf16[8,64,256]{2,1,0:T(8,128)(2,1)S(1)} all-to-all(bf16[8,64,256]{2,1,0:T(8,128)(2,1)S(1)} %convolution_convert_fusion.2), channel_id=1, replica_groups=mesh['space'=64,'snap'=8] {'snap'}, dimensions={0} | all-to-all | bytes 524288 | tf_op jit(solution)/shard_map/all_to_all | solution.py:13
  92.2 22.7 %all_to_all.36 = f32[8,8,256]{2,1,0:T(8,128)S(1)} all-to-all(f32[8,8,256]{2,1,0:T(8,128)S(1)} %bitcast.84), channel_id=1, replica_groups={{0,8,16,24,256,264,272,280},{32,40,48,56,288,296,304,312},{64,72,80,88,..., dimensions={0} | all-to-all | bytes 131072 | tf_op jit(solution)/shard_map/all_to_all | solution.py:13
  114.9 17.3 %all_to_all.37 = f32[8,8,256]{2,1,0:T(8,128)S(1)} all-to-all(f32[8,8,256]{2,1,0:T(8,128)S(1)} %broadcast_in_dim.42), channel_id=1, replica_groups={{0,32,64,96,128,160,192,224},{8,40,72,104,136,168,200,232},{16,48,80,11..., dimensions={0} | all-to-all | bytes 131072 | tf_op jit(solution)/shard_map/all_to_all | solution.py:13
  132.8 5.7 %all-to-all-start.6 = ((f32[8,8,256]{2,1,0:T(8,128)}), f32[8,8,256]{2,1,0:T(8,128)S(1)}, u32[]{:S(2)}, u32[]{:S(2)}) async-start(f32[8,8,256]{2,1,0:T(8,128)} %broadcast_in_dim.43), calls=%async_computation.6 | async-start | bytes 131072 | tf_op jit(solution)/shard_map/all_to_all | solution.py:13
  139.2 5.0 %all-to-all-done.6 = f32[8,8,256]{2,1,0:T(8,128)S(1)} async-done(((f32[8,8,256]{2,1,0:T(8,128)}), f32[8,8,256]{2,1,0:T(8,128)S(1)}, u32[]{:S(2)}, u32[]{:S(2)}) %all-to-all-start.6) | async-done | bytes 65568 | tf_op jit(solution)/shard_map/all_to_all | solution.py:13
  (57 shorter events, 12.8 us)
Async XLA Ops:
  0.6 1.4 copy-start
  4.7 6.0 %copy-start.9 = (s32[1,4,6]{2,1,0:T(4,128)S(1)}, s32[1,4,6]{2,1,0:T(4,128)}, u32[]{:S(2)}) copy-start(s32[1,4,6]{2,1,0:T(4,128)} %param.15) | copy-start | bytes 292
  4.7 6.1 %copy-start.8 = (s32[24,5]{0,1:T(8,128)S(1)}, s32[24,5]{0,1:T(8,128)}, u32[]{:S(2)}) copy-start(s32[24,5]{0,1:T(8,128)} %param.14) | copy-start | bytes 1444
  4.7 25.2 %all-to-all-start = ((bf16[8,32,3072]{2,1,0:T(8,128)(2,1)}), bf16[8,32,3072]{2,1,0:T(8,128)(2,1)S(1)}, u32[]{:S(2)}, u32[]{:S(2)}) async-start(bf16[8,32,3072]{2,1,0:T(8,128)(2,1)} %bitcast.75), calls=%async_computation | async-start | bytes 3145728 | tf_op jit(solution)/shard_map/all_to_all | solution.py:13
  11.5 3.1 %copy-start.11 = (s32[24]{0:T(128)S(1)}, s32[24]{0:T(128)}, u32[]{:S(2)}) copy-start(s32[24]{0:T(128)} %param.13) | copy-start | bytes 292
  11.5 3.2 %copy-start.7 = (bf16[256,256]{1,0:T(8,128)(2,1)S(1)}, bf16[256,256]{1,0:T(8,128)(2,1)}, u32[]{:S(2)}) copy-start(bf16[256,256]{1,0:T(8,128)(2,1)} %param.11) | copy-start | bytes 393220
  29.9 1.2 copy-start.1
  31.0 37.9 %all-to-all-start.2 = ((bf16[8,256,384]{1,2,0:T(8,128)(2,1)}), bf16[8,256,384]{1,2,0:T(8,128)(2,1)S(1)}, u32[]{:S(2)}, u32[]{:S(2)}) async-start(bf16[8,256,384]{1,2,0:T(8,128)(2,1)} %fusion), calls=%async_computation.2 | async-start | bytes 3145728 | tf_op jit(solution)/shard_map/all_to_all | solution.py:13
  37.1 21.8 %copy-start.3 = (bf16[32,3072]{1,0:T(8,128)(2,1)}, bf16[32,3072]{1,0:T(8,128)(2,1)S(1)}, u32[]{:S(2)}) copy-start(bf16[32,3072]{1,0:T(8,128)(2,1)S(1)} %reduce_sum.51) | copy-start | bytes 589828
  37.2 21.8 %copy-start.2 = (bf16[32,24,128]{2,0,1:T(8,128)(2,1)}, bf16[32,24,128]{2,0,1:T(8,128)(2,1)S(1)}, u32[]{:S(2)}) copy-start(bf16[32,24,128]{2,0,1:T(8,128)(2,1)S(1)} %copy_bitcast_fusion.2) | copy-start | bytes 589828
  40.2 17.8 %collective-permute-start = (bf16[32,6,128]{2,0,1:T(8,128)(2,1)}, bf16[32,6,128]{2,0,1:T(8,128)(2,1)}, u32[]{:S(2)}, u32[]{:S(2)}) collective-permute-start(bf16[32,6,128]{2,0,1:T(8,128)(2,1)} %get-tuple-element.4), channel_id=1, source_target_pairs={{0,16},{8,24},{16,32},{24,40},{32,48},{40,56},{48,64},{56,72},{64,... | collective-permute-start | bytes 147464 | tf_op jit(solution)/shard_map/ppermute | solution.py:19
  47.3 10.6 %collective-permute-start.3 = (bf16[32,6,128]{2,0,1:T(8,128)(2,1)}, bf16[32,6,128]{2,0,1:T(8,128)(2,1)}, u32[]{:S(2)}, u32[]{:S(2)}) collective-permute-start(bf16[32,6,128]{2,0,1:T(8,128)(2,1)} %get-tuple-element.5), channel_id=1, source_target_pairs={{16,0},{24,8},{32,16},{40,24},{48,32},{56,40},{64,48},{72,56},{80,... | collective-permute-start | bytes 147464 | tf_op jit(solution)/shard_map/ppermute | solution.py:19
  48.6 9.3 %collective-permute-start.2 = (bf16[32,6,128]{2,0,1:T(8,128)(2,1)}, bf16[32,6,128]{2,0,1:T(8,128)(2,1)}, u32[]{:S(2)}, u32[]{:S(2)}) collective-permute-start(bf16[32,6,128]{2,0,1:T(8,128)(2,1)} %get-tuple-element.6), channel_id=1, source_target_pairs={{8,0},{16,8},{24,16},{32,24},{40,32},{48,40},{56,48},{64,56},{72,6... | collective-permute-start | bytes 147464 | tf_op jit(solution)/shard_map/ppermute | solution.py:19
  52.4 5.6 %collective-permute-start.1 = (bf16[32,6,128]{2,0,1:T(8,128)(2,1)}, bf16[32,6,128]{2,0,1:T(8,128)(2,1)}, u32[]{:S(2)}, u32[]{:S(2)}) collective-permute-start(bf16[32,6,128]{2,0,1:T(8,128)(2,1)} %get-tuple-element.7), channel_id=1, source_target_pairs={{0,8},{8,16},{16,24},{24,32},{32,40},{40,48},{48,56},{56,64},{64,7... | collective-permute-start | bytes 147464 | tf_op jit(solution)/shard_map/ppermute | solution.py:19
  60.0 1.7 %copy-start.10 = (pred[24,5]{1,0:T(8,128)(4,1)S(1)}, pred[24,5]{1,0:T(8,128)(4,1)}, u32[]{:S(2)}) copy-start(pred[24,5]{1,0:T(8,128)(4,1)} %copy.41) | copy-start | bytes 364
  61.6 5.5 %copy-start.4 = (bf16[32,3072]{1,0:T(8,128)(2,1)S(1)}, bf16[32,3072]{1,0:T(8,128)(2,1)}, u32[]{:S(2)}) copy-start(bf16[32,3072]{1,0:T(8,128)(2,1)} %copy-done.3) | copy-start | bytes 589828
  65.5 0.7 copy-start.5
  68.9 13.2 %all-to-all-start.1 = ((bf16[8,64,384]{2,1,0:T(8,128)(2,1)}), bf16[8,64,384]{2,1,0:T(8,128)(2,1)S(1)}, u32[]{:S(2)}, u32[]{:S(2)}) async-start(bf16[8,64,384]{2,1,0:T(8,128)(2,1)} %bitcast.74), calls=%async_computation.1 | async-start | bytes 786432 | tf_op jit(solution)/shard_map/all_to_all | solution.py:13
  75.2 63.4 %copy-start.6 = (bf16[24,32,128]{2,1,0:T(8,128)(2,1)S(1)}, bf16[24,32,128]{2,1,0:T(8,128)(2,1)}, u32[]{:S(2)}) copy-start(bf16[24,32,128]{2,1,0:T(8,128)(2,1)} %copy-done.5) | copy-start | bytes 589828
  132.8 11.4 %all-to-all-start.6 = ((f32[8,8,256]{2,1,0:T(8,128)}), f32[8,8,256]{2,1,0:T(8,128)S(1)}, u32[]{:S(2)}, u32[]{:S(2)}) async-start(f32[8,8,256]{2,1,0:T(8,128)} %broadcast_in_dim.43), calls=%async_computation.6 | async-start | bytes 131072 | tf_op jit(solution)/shard_map/all_to_all | solution.py:13

commit v2 on v1

v2 whole, which is shorter than its diff:
```python
import functools
import math

import jax
import jax.numpy as jnp
from jax import lax
from jax.experimental import pallas as pl
from jax.experimental.pallas import tpu as pltpu
from jax.sharding import PartitionSpec as P

F32 = jnp.float32
BF16 = jnp.bfloat16
STEPS = (2, 1, -1, -2)
NEAR = 4
PARTS = 6
PAIR = 2


def exchange(tiles, axis, groups=None):
    return lax.all_to_all(tiles, axis, 0, 0, tiled=True, axis_index_groups=groups)


def passed_along(value, axis, steps):
    count = lax.axis_size(axis)
    first, last = (max(0, -steps), min(count, count - steps))
    return lax.ppermute(value, axis, [(source, source + steps) for source in range(first, last)])


def z_groups(space):
    half, depth = space // 2, space // NEAR
    along = [[h * half + z * 2 + c for z in range(depth)] for h in range(2) for c in range(2)]
    across = [[h * half + z * 2 + c for h in range(2) for c in range(2)] for z in range(depth)]
    return along, across


def vmem():
    return pl.BlockSpec(memory_space=pltpu.VMEM)


def smem():
    return pl.BlockSpec(memory_space=pltpu.SMEM)


def sum_kernel(send_ref, tiles_ref, primal_ref, *out_refs):
    ways = tiles_ref.shape[0]
    total = tiles_ref[0].astype(F32)
    for j in range(1, ways):
        total = total + tiles_ref[j].astype(F32)
    primal_ref[...] = total.astype(BF16)
    size = out_refs[0].shape[2]
    for d, out_ref in enumerate(out_refs):
        for t in range(out_ref.shape[0]):
            start = pl.multiple_of(send_ref[d, t] * size, size)
            out_ref[t] = primal_ref[:, pl.ds(start, size)]


def sum_and_pick(tiles, ghost_send, size):
    ways, share, unknowns = tiles.shape
    lists, length = ghost_send.shape
    return pl.pallas_call(
        sum_kernel,
        out_shape=[jax.ShapeDtypeStruct((share, unknowns), BF16)]
        + [jax.ShapeDtypeStruct((length, share, size), BF16)] * lists,
        in_specs=[smem(), vmem()],
        out_specs=[vmem()] * (1 + lists),
        compiler_params=pltpu.CompilerParams(vmem_limit_bytes=8 << 20),
    )(ghost_send, tiles)


def apply_kernel(counts_ref, cols_ref, primal_ref, *refs):
    *ghost_refs, op_hbm, applied_ref, both_ref, held, op_ref, sems = refs
    rows, slots, size, _ = op_ref.shape
    count = sems.shape[0]
    part = rows // count
    copies = []
    for i in range(count):
        cut = pl.ds(i * part, part)
        copies.append(pltpu.make_async_copy(op_hbm.at[cut], op_ref.at[cut], sems.at[i]))
        copies[-1].start()
    share = primal_ref.shape[0]
    ways, _, piece = both_ref.shape
    for b in range(rows):
        held[b] = primal_ref[:, b * size : (b + 1) * size]
    at = rows
    for ghost_ref in ghost_refs:
        length = ghost_ref.shape[0]
        held[at : at + length] = ghost_ref[...]
        at += length
    per = piece // size
    for r in range(rows):
        if r % part == 0:
            copies[r // part].wait()
        total = None
        for k in range(slots):
            block = held[cols_ref[r, k]]
            block = jnp.where(k < counts_ref[r], block, jnp.zeros_like(block))
            term = lax.dot_general(
                block, op_ref[r, k], (((1,), (1,)), ((), ())), preferred_element_type=F32
            )
            total = term if total is None else total + term
        out = total.astype(BF16)
        applied_ref[:, r * size : (r + 1) * size] = out
        both_ref[r // per, :share, (r % per) * size : (r % per + 1) * size] = out
    for w in range(ways):
        both_ref[w, share:, :] = primal_ref[:, w * piece : (w + 1) * piece]


def applied_and_laid_out(counts, cols, primal, ghosts, op_blocks, ways):
    share, unknowns = primal.shape
    rows, slots, size, _ = op_blocks.shape
    held = rows + sum(g.shape[0] for g in ghosts)
    return pl.pallas_call(
        apply_kernel,
        out_shape=[
            jax.ShapeDtypeStruct((share, unknowns), BF16),
            jax.ShapeDtypeStruct((ways, 2 * share, unknowns // ways), BF16),
        ],
        in_specs=[smem(), smem()]
        + [vmem()] * (1 + len(ghosts))
        + [pl.BlockSpec(memory_space=pltpu.HBM)],
        out_specs=[vmem(), vmem()],
        scratch_shapes=[
            pltpu.VMEM((held, share, size), BF16),
            pltpu.VMEM(op_blocks.shape, BF16),
            pltpu.SemaphoreType.DMA((PARTS,)),
        ],
        compiler_params=pltpu.CompilerParams(vmem_limit_bytes=60 << 20),
    )(counts, cols, primal, *ghosts, op_blocks)


def per_device(
    snaps_primal, snaps_adjoint, coef_primal, coef_adjoint, op_blocks, counts, col_index, ghost_send
):
    ways, space = lax.axis_size("snap"), lax.axis_size("space")
    runs = ways // PAIR
    modes = coef_primal.shape[1]
    share = modes // ways
    unknowns = snaps_primal.shape[1]
    piece = unknowns // ways
    size = op_blocks.shape[2]
    along_z, across_z = z_groups(space)
    flat_groups = [[p * ways + s for s in range(ways) for p in group] for group in across_z]
    along_x = [[x * PAIR + y for x in range(runs)] for y in range(PAIR)]

    primal_part = jnp.einsum("mr,ms->rs", coef_primal, snaps_primal, preferred_element_type=F32)
    primal_tiles = exchange(primal_part.astype(BF16).reshape(ways, share, unknowns), "snap")

    adjoint_part = jnp.einsum("mr,ms->rs", coef_adjoint, snaps_adjoint, preferred_element_type=F32)
    adjoint_tiles = jnp.moveaxis(adjoint_part.astype(BF16).reshape(modes, runs, PAIR * piece), 1, 0)
    primal, *outgoing = sum_and_pick(primal_tiles, ghost_send[0], size)
    adjoint_tiles, primal = lax.optimization_barrier((adjoint_tiles, primal))
    adjoint_tiles = exchange(adjoint_tiles, "snap", along_x)
    adjoint_run = adjoint_tiles.astype(F32).sum(axis=0)
    y = lax.axis_index("snap") % PAIR
    own = lax.dynamic_slice_in_dim(adjoint_run, y * piece, piece, axis=1)
    other = lax.dynamic_slice_in_dim(adjoint_run, (1 - y) * piece, piece, axis=1).astype(BF16)
    arrived = lax.ppermute(other, "snap", [(s, s ^ 1) for s in range(ways)])
    adjoint = (own + arrived.astype(F32)).astype(BF16)

    ghosts = [passed_along(o, "space", step) for o, step in zip(outgoing, STEPS)]
    applied, both = applied_and_laid_out(counts, col_index, primal, ghosts, op_blocks, ways)

    both = exchange(both, "snap")
    products = jnp.einsum("was,bs->wab", both, adjoint, preferred_element_type=F32).astype(BF16)
    rows = 2 * share // NEAR
    tiles = exchange(products.reshape(ways * NEAR, rows, modes), ("space", "snap"), flat_groups)
    mine = tiles.astype(F32).sum(axis=0).astype(BF16)
    every = exchange(jnp.broadcast_to(mine[None], (space // NEAR, rows, modes)), "space", along_z)
    factor = 1.0 / math.sqrt(unknowns * space)
    mine = every.astype(F32).sum(axis=0) * factor
    total = exchange(jnp.broadcast_to(mine[None], (NEAR, rows, modes)), "space", across_z)
    total = total.reshape(2 * share, modes)
    return (primal, applied, total[:share].T, total[share:].T)


def solution(mesh):
    placed = (
        P("snap", "space"),
        P("snap", "space"),
        P("snap", None),
        P("snap", None),
        P("space", None, None, None),
        P("space"),
        P("space", None),
        P("space", None, None),
    )
    return jax.shard_map(
        per_device,
        mesh=mesh,
        in_specs=placed,
        out_specs=(P("snap", "space"), P("snap", "space"), P(None, "snap"), P(None, "snap")),
        check_vma=False,
    )
```

time: 146 us -> 132 us (0.904)
  local copies, waits for them, and re-layouts: 14.6 us -> 5.57 us
  other arithmetic: 7.77 us -> 0.29 us
  Pallas kernels: 0 us -> 7.27 us
  matrix products: 10.9 us -> 5.96 us
  starting transfers between devices: 37.9 us -> 33.5 us
  blocking collectives: 48.8 us -> 51.6 us
  waiting for transfers between devices: 24 us -> 26.7 us
    all_to_all x4 -> x3, starting transfers between devices: 21.5 us -> 14.2 us  [exchange(): lax.all_to_all(tiles, axis, 0, 0, tiled=True, axis_index_groups=groups)]
    pallas_call x0 -> x2, Pallas kernels: none -> 7.27 us  [the longest x1 5.71 us: applied_and_laid_out(): pl.pallas_call(apply_kernel, out_shape=[jax.ShapeDtypeStruct((share, unkn...]
    all_to_all x4 -> x3, waiting for transfers between devices: 23.9 us -> 18.5 us  [exchange(): lax.all_to_all(tiles, axis, 0, 0, tiled=True, axis_index_groups=groups)]
    dot_general x2 -> x1, matrix products: 7.04 us -> 2 us  [per_device(): jnp.einsum('mr,ms->rs', coef_adjoint, snaps_adjoint, preferred_element_ty...]
    ppermute x0 -> x1, waiting for transfers between devices: none -> 4.69 us  [per_device(): arrived = lax.ppermute(other, 'snap', [(s, s ^ 1) for s in range(ways)])]
    ppermute x0 -> x1, starting transfers between devices: none -> 3.37 us  [per_device(): arrived = lax.ppermute(other, 'snap', [(s, s ^ 1) for s in range(ways)])]
    ppermute x4, waiting for transfers between devices: 0.13 us -> 3.5 us  [passed_along(): lax.ppermute(value, axis, [(source, source + steps) for source in range(f...]
    gather x2 -> x0, local copies, waits for them, and re-layouts: 2.91 us -> none  [the longest x1 1.66 us: per_device(): picked = jnp.take(extended, col_index, axis=1)]
  transfers between devices with their start and end apart: 8 -> 8, of which waited for: 4 -> 5; matrix products, arithmetic and copies ran while one was open for 17% -> 3% of each run, Pallas kernels for 0% -> 4%
where the time goes in v2:
time: 132 us
  blocking collectives  51.6 us (39%)
  starting transfers between devices  33.5 us (25%)
  waiting for transfers between devices  26.7 us (20%)
  Pallas kernels  7.27 us (6%)
  matrix products  5.96 us (5%)
  local copies, waits for them, and re-layouts  5.57 us (4%)
    all_to_all x3, blocking collectives, exchange(): lax.all_to_all(tiles, axis, 0, 0, tiled=True, axis_index_groups=groups)  51.6 us
    all_to_all x3, waiting for transfers between devices, exchange(): lax.all_to_all(tiles, axis, 0, 0, tiled=True, axis_index_groups=groups)  18.5 us
    ppermute x4, starting transfers between devices, passed_along(): lax.ppermute(value, axis, [(source, source + steps) for source in range(f...  15.9 us
    all_to_all x3, starting transfers between devices, exchange(): lax.all_to_all(tiles, axis, 0, 0, tiled=True, axis_index_groups=groups)  14.2 us
    pallas_call x1, Pallas kernels, applied_and_laid_out(): pl.pallas_call(apply_kernel, out_shape=[jax.ShapeDtypeStruct((share, unkn...  5.71 us
    ppermute x1, waiting for transfers between devices, per_device(): arrived = lax.ppermute(other, 'snap', [(s, s ^ 1) for s in range(ways)])  4.69 us
    unnamed x19, local copies, waits for them, and re-layouts  3.63 us
    ppermute x4, waiting for transfers between devices, passed_along(): lax.ppermute(value, axis, [(source, source + steps) for source in range(f...  3.5 us
  transfers between devices with their start and end apart: 8, of which 5 were waited for; matrix products, arithmetic and copies ran while one was open for 3% of the time, Pallas kernels for 4%

profile of v2, /device:TPU:1, one launch (start us, length us, event | category | flops | bytes accessed | tf_op | source)
XLA Modules:
  0.0 131.7 jit_solution(874413234436916717)
XLA Ops:
  0.6 1.4 %copy-done = bf16[256,3072]{1,0:T(8,128)(2,1)S(1)} copy-done((bf16[256,3072]{1,0:T(8,128)(2,1)S(1)}, bf16[256,3072]{1,0:T(8,128)(2,1)}, u32[]{:S(2)}) %copy-start) | copy-done | bytes 1572888
  2.0 2.6 %convolution_convert_fusion = bf16[256,3072]{1,0:T(8,128)(2,1)} fusion(bf16[256,256]{1,0:T(8,128)(2,1)} %param.10, bf16[256,3072]{1,0:T(8,128)(2,1)S(1)} %copy-done), kind=kOutput, calls=%fused_computation | convolution fusion | flops 403439616 | bytes 3276800 | tf_op jit(solution)/shard_map/mr,ms->rs/dot_general | solution.py:145
  4.7 6.0 %all-to-all-start = ((bf16[8,32,3072]{2,1,0:T(8,128)(2,1)}), bf16[8,32,3072]{2,1,0:T(8,128)(2,1)S(1)}, u32[]{:S(2)}, u32[]{:S(2)}) async-start(bf16[8,32,3072]{2,1,0:T(8,128)(2,1)} %bitcast.26), calls=%async_computation | async-start | bytes 3145728 | tf_op jit(solution)/shard_map/all_to_all | solution.py:20
  10.7 2.0 %convolution_convert_fusion.1 = bf16[256,3072]{1,0:T(8,128)(2,1)S(1)} fusion(bf16[256,256]{1,0:T(8,128)(2,1)S(1)} %copy-done.3, bf16[256,3072]{1,0:T(8,128)(2,1)} %param.9), kind=kOutput, calls=%fused_computation.1 | convolution fusion | flops 403439616 | bytes 3276800 | tf_op jit(solution)/shard_map/mr,ms->rs/dot_general | solution.py:148
  12.7 1.3 copy.19
  14.0 15.9 %all-to-all-done.tiles_ref = bf16[8,32,3072]{2,1,0:T(8,128)(2,1)S(1)} async-done(((bf16[8,32,3072]{2,1,0:T(8,128)(2,1)}), bf16[8,32,3072]{2,1,0:T(8,128)(2,1)S(1)}, u32[]{:S(2)}, u32[]{:S(2)}) %all-to-all-start) | async-done | bytes 1572896 | tf_op jit(solution)/shard_map/all_to_all | solution.py:20
  29.9 1.6 %shard_map.111 = (bf16[32,3072]{1,0:T(8,128)(2,1)}, bf16[6,32,128]{2,1,0:T(8,128)(2,1)S(1)}, bf16[6,32,128]{2,1,0:T(8,128)(2,1)S(1)}, bf16[6,32,128]{2,1,0:T(8,128)(2,1)S(1)}, bf16[6,32,128]{2,1,0:T(8,128)(2,1)S(1)}) custom-call(s32[4,6]{1,0:T(4,128)S(1)} %bitcast.24, bf16[8,32,3072]{2,1,0:T(8,128)(2,1)S(1)} %all-to-all-done.tiles_ref), custom_call_target="tpu_custom_call" | custom-call | tf_op jit(solution)/shard_map/pallas_call | solution.py:60
  31.4 3.7 %all-to-all-start.2 = ((bf16[4,256,768]{2,1,0:T(8,128)(2,1)}), bf16[4,256,768]{2,1,0:T(8,128)(2,1)S(1)}, u32[]{:S(2)}, u32[]{:S(2)}) async-start(bf16[4,256,768]{2,1,0:T(8,128)(2,1)} %bitcast.25), calls=%async_computation.2 | async-start | bytes 3145728 | tf_op jit(solution)/shard_map/all_to_all | solution.py:20
  35.1 7.4 %collective-permute-start = (bf16[6,32,128]{2,1,0:T(8,128)(2,1)S(1)}, bf16[6,32,128]{2,1,0:T(8,128)(2,1)S(1)}, u32[]{:S(2)}, u32[]{:S(2)}) collective-permute-start(bf16[6,32,128]{2,1,0:T(8,128)(2,1)S(1)} %get-tuple-element.15), channel_id=1, source_target_pairs={{0,16},{8,24},{16,32},{24,40},{32,48},{40,56},{48,64},{56,72},{64,... | collective-permute-start | bytes 147464 | tf_op jit(solution)/shard_map/ppermute | solution.py:26
  42.5 5.3 %collective-permute-start.1 = (bf16[6,32,128]{2,1,0:T(8,128)(2,1)S(1)}, bf16[6,32,128]{2,1,0:T(8,128)(2,1)S(1)}, u32[]{:S(2)}, u32[]{:S(2)}) collective-permute-start(bf16[6,32,128]{2,1,0:T(8,128)(2,1)S(1)} %get-tuple-element.16), channel_id=1, source_target_pairs={{0,8},{8,16},{16,24},{24,32},{32,40},{40,48},{48,56},{56,64},{64,7... | collective-permute-start | bytes 147464 | tf_op jit(solution)/shard_map/ppermute | solution.py:26
  47.9 1.9 %collective-permute-start.2 = (bf16[6,32,128]{2,1,0:T(8,128)(2,1)S(1)}, bf16[6,32,128]{2,1,0:T(8,128)(2,1)S(1)}, u32[]{:S(2)}, u32[]{:S(2)}) collective-permute-start(bf16[6,32,128]{2,1,0:T(8,128)(2,1)S(1)} %get-tuple-element.17), channel_id=1, source_target_pairs={{8,0},{16,8},{24,16},{32,24},{40,32},{48,40},{56,48},{64,56},{72,6... | collective-permute-start | bytes 147464 | tf_op jit(solution)/shard_map/ppermute | solution.py:26
  49.8 1.3 collective-permute-start.3
  51.8 1.7 %collective-permute-done.2.refs_2_ = bf16[6,32,128]{2,1,0:T(8,128)(2,1)S(1)} collective-permute-done((bf16[6,32,128]{2,1,0:T(8,128)(2,1)S(1)}, bf16[6,32,128]{2,1,0:T(8,128)(2,1)S(1)}, u32[]{:S(2)}, u32[]{:S(2)}) %collective-permute-start.2) | collective-permute-done | bytes 49184 | tf_op jit(solution)/shard_map/ppermute | solution.py:26
  53.6 1.8 %collective-permute-done.3.refs_3_ = bf16[6,32,128]{2,1,0:T(8,128)(2,1)S(1)} collective-permute-done((bf16[6,32,128]{2,1,0:T(8,128)(2,1)S(1)}, bf16[6,32,128]{2,1,0:T(8,128)(2,1)S(1)}, u32[]{:S(2)}, u32[]{:S(2)}) %collective-permute-start.3) | collective-permute-done | bytes 49184 | tf_op jit(solution)/shard_map/ppermute | solution.py:26
  56.0 5.7 %shard_map.112 = (bf16[32,3072]{1,0:T(8,128)(2,1)}, bf16[8,64,384]{2,1,0:T(8,128)(2,1)}) custom-call(s32[24]{0:T(128)} %counts_ref.1, s32[24,5]{1,0:T(8,128)} %copy.16.cols_ref, bf16[32,3072]{1,0:T(8,128)(2,1)} %get-tuple-element.9.primal_ref, bf16[6,32,128]{2,1,0:T(8,128)(2,1)} %copy-done.4, bf16[6,32,128]{2,1,0:T(8,128)(2,1)} %copy-done.5, ...), custom_call_target="tpu_custom_call" | custom-call | tf_op jit(solution)/shard_map/pallas_call | solution.py:112
  61.7 4.5 %all-to-all-start.1 = ((bf16[8,64,384]{2,1,0:T(8,128)(2,1)}), bf16[8,64,384]{2,1,0:T(8,128)(2,1)S(1)}, u32[]{:S(2)}, u32[]{:S(2)}) async-start(bf16[8,64,384]{2,1,0:T(8,128)(2,1)} %get-tuple-element.20), calls=%async_computation.1 | async-start | bytes 786432 | tf_op jit(solution)/shard_map/all_to_all | solution.py:20
  66.4 0.9 copy-done.2
  67.4 3.4 %collective-permute-start.4 = (bf16[256,384]{1,0:T(8,128)(2,1)S(1)}, bf16[256,384]{1,0:T(8,128)(2,1)S(1)}, u32[]{:S(2)}, u32[]{:S(2)}) collective-permute-start(bf16[256,384]{1,0:T(8,128)(2,1)S(1)} %dynamic-slice_convert_fusion), channel_id=1, source_target_pairs={{0,1},{1,0},{2,3},{3,2},{4,5},{5,4},{6,7},{7,6},{8,9},{9,8},{10,11... | collective-permute-start | bytes 589832 | tf_op jit(solution)/shard_map/ppermute | solution.py:157
  70.7 2.6 %all-to-all-done.1 = bf16[8,64,384]{2,1,0:T(8,128)(2,1)S(1)} async-done(((bf16[8,64,384]{2,1,0:T(8,128)(2,1)}), bf16[8,64,384]{2,1,0:T(8,128)(2,1)S(1)}, u32[]{:S(2)}, u32[]{:S(2)}) %all-to-all-start.1) | async-done | bytes 393248 | tf_op jit(solution)/shard_map/all_to_all | solution.py:20
  73.3 4.7 %collective-permute-done.4 = bf16[256,384]{1,0:T(8,128)(2,1)S(1)} collective-permute-done((bf16[256,384]{1,0:T(8,128)(2,1)S(1)}, bf16[256,384]{1,0:T(8,128)(2,1)S(1)}, u32[]{:S(2)}, u32[]{:S(2)}) %collective-permute-start.4) | collective-permute-done | bytes 196640 | tf_op jit(solution)/shard_map/ppermute | solution.py:157
  78.0 1.3 %convolution_convert_fusion.2 = bf16[8,64,256]{2,1,0:T(8,128)(2,1)S(1)} fusion(bf16[8,64,384]{2,1,0:T(8,128)(2,1)S(1)} %all-to-all-done.1, bf16[256,384]{1,0:T(8,128)(2,1)S(1)} %collective-permute-done.4, f32[256,768]{1,0:T(8,128)} %copy-done.2, s32[]{:T(128)S(6)} %select_n.14), kind=kOutput, calls=%fused_computation.4 | convolution fusion | flops 101089280 | bytes 1245188 | tf_op jit(solution)/shard_map/was,bs->wab/dot_general | solution.py:164
  79.3 19.8 %all_to_all.30 = bf16[32,16,256]{2,1,0:T(8,128)(2,1)S(1)} all-to-all(bf16[32,16,256]{2,1,0:T(8,128)(2,1)S(1)} %bitcast.28), channel_id=1, replica_groups={{0,8,256,264,1,9,257,265,2,10,258,266,3,11,259,267,4,12,260,268,5,13,26..., dimensions={0} | all-to-all | bytes 524288 | tf_op jit(solution)/shard_map/all_to_all | solution.py:20
  99.2 21.3 %all_to_all.31 = bf16[16,16,256]{2,1,0:T(8,128)(2,1)S(1)} all-to-all(bf16[16,16,256]{2,1,0:T(8,128)(2,1)S(1)} %broadcast_in_dim.4), channel_id=1, replica_groups={{0,16,32,48,64,80,96,112,128,144,160,176,192,208,224,240},{8,24,40,56,7..., dimensions={0} | all-to-all | bytes 262144 | tf_op jit(solution)/shard_map/all_to_all | solution.py:20
  120.5 10.5 %all_to_all.32 = f32[4,16,256]{2,1,0:T(8,128)S(1)} all-to-all(f32[4,16,256]{2,1,0:T(8,128)S(1)} %broadcast_in_dim.5), channel_id=1, replica_groups={{0,8,256,264},{16,24,272,280},{32,40,288,296},{48,56,304,312},{64,72,32..., dimensions={0} | all-to-all | bytes 131072 | tf_op jit(solution)/shard_map/all_to_all | solution.py:20
  (28 shorter events, 2.3 us)
Async XLA Ops:
  0.6 1.4 %copy-start = (bf16[256,3072]{1,0:T(8,128)(2,1)S(1)}, bf16[256,3072]{1,0:T(8,128)(2,1)}, u32[]{:S(2)}) copy-start(bf16[256,3072]{1,0:T(8,128)(2,1)} %param.8) | copy-start | bytes 4718596
  4.7 6.0 %copy-start.3 = (bf16[256,256]{1,0:T(8,128)(2,1)S(1)}, bf16[256,256]{1,0:T(8,128)(2,1)}, u32[]{:S(2)}) copy-start(bf16[256,256]{1,0:T(8,128)(2,1)} %param.11) | copy-start | bytes 393220
  4.7 25.2 %all-to-all-start = ((bf16[8,32,3072]{2,1,0:T(8,128)(2,1)}), bf16[8,32,3072]{2,1,0:T(8,128)(2,1)S(1)}, u32[]{:S(2)}, u32[]{:S(2)}) async-start(bf16[8,32,3072]{2,1,0:T(8,128)(2,1)} %bitcast.26), calls=%async_computation | async-start | bytes 3145728 | tf_op jit(solution)/shard_map/all_to_all | solution.py:20
  12.7 17.2 %copy-start.1 = (s32[1,4,6]{2,1,0:T(4,128)S(1)}, s32[1,4,6]{2,1,0:T(4,128)}, u32[]{:S(2)}) copy-start(s32[1,4,6]{2,1,0:T(4,128)} %param.15) | copy-start | bytes 292
  31.4 19.7 %copy-start.8 = (s32[24,5]{0,1:T(8,128)S(1)}, s32[24,5]{0,1:T(8,128)}, u32[]{:S(2)}) copy-start(s32[24,5]{0,1:T(8,128)} %param.14) | copy-start | bytes 1444
  31.4 30.3 %all-to-all-start.2 = ((bf16[4,256,768]{2,1,0:T(8,128)(2,1)}), bf16[4,256,768]{2,1,0:T(8,128)(2,1)S(1)}, u32[]{:S(2)}, u32[]{:S(2)}) async-start(bf16[4,256,768]{2,1,0:T(8,128)(2,1)} %bitcast.25), calls=%async_computation.2 | async-start | bytes 3145728 | tf_op jit(solution)/shard_map/all_to_all | solution.py:20
  35.1 16.7 %collective-permute-start = (bf16[6,32,128]{2,1,0:T(8,128)(2,1)S(1)}, bf16[6,32,128]{2,1,0:T(8,128)(2,1)S(1)}, u32[]{:S(2)}, u32[]{:S(2)}) collective-permute-start(bf16[6,32,128]{2,1,0:T(8,128)(2,1)S(1)} %get-tuple-element.15), channel_id=1, source_target_pairs={{0,16},{8,24},{16,32},{24,40},{32,48},{40,56},{48,64},{56,72},{64,... | collective-permute-start | bytes 147464 | tf_op jit(solution)/shard_map/ppermute | solution.py:26
  42.5 9.3 %collective-permute-start.1 = (bf16[6,32,128]{2,1,0:T(8,128)(2,1)S(1)}, bf16[6,32,128]{2,1,0:T(8,128)(2,1)S(1)}, u32[]{:S(2)}, u32[]{:S(2)}) collective-permute-start(bf16[6,32,128]{2,1,0:T(8,128)(2,1)S(1)} %get-tuple-element.16), channel_id=1, source_target_pairs={{0,8},{8,16},{16,24},{24,32},{32,40},{40,48},{48,56},{56,64},{64,7... | collective-permute-start | bytes 147464 | tf_op jit(solution)/shard_map/ppermute | solution.py:26
  47.9 5.7 %collective-permute-start.2 = (bf16[6,32,128]{2,1,0:T(8,128)(2,1)S(1)}, bf16[6,32,128]{2,1,0:T(8,128)(2,1)S(1)}, u32[]{:S(2)}, u32[]{:S(2)}) collective-permute-start(bf16[6,32,128]{2,1,0:T(8,128)(2,1)S(1)} %get-tuple-element.17), channel_id=1, source_target_pairs={{8,0},{16,8},{24,16},{32,24},{40,32},{48,40},{56,48},{64,56},{72,6... | collective-permute-start | bytes 147464 | tf_op jit(solution)/shard_map/ppermute | solution.py:26
  49.8 5.5 %collective-permute-start.3 = (bf16[6,32,128]{2,1,0:T(8,128)(2,1)S(1)}, bf16[6,32,128]{2,1,0:T(8,128)(2,1)S(1)}, u32[]{:S(2)}, u32[]{:S(2)}) collective-permute-start(bf16[6,32,128]{2,1,0:T(8,128)(2,1)S(1)} %get-tuple-element.18), channel_id=1, source_target_pairs={{16,0},{24,8},{32,16},{40,24},{48,32},{56,40},{64,48},{72,56},{80,... | collective-permute-start | bytes 147464 | tf_op jit(solution)/shard_map/ppermute | solution.py:26
  51.8 3.5 %copy-start.4 = (bf16[6,32,128]{2,1,0:T(8,128)(2,1)}, bf16[6,32,128]{2,1,0:T(8,128)(2,1)S(1)}, u32[]{:S(2)}) copy-start(bf16[6,32,128]{2,1,0:T(8,128)(2,1)S(1)} %collective-permute-done.refs_0_) | copy-start | bytes 147460
  51.8 3.5 %copy-start.5 = (bf16[6,32,128]{2,1,0:T(8,128)(2,1)}, bf16[6,32,128]{2,1,0:T(8,128)(2,1)S(1)}, u32[]{:S(2)}) copy-start(bf16[6,32,128]{2,1,0:T(8,128)(2,1)S(1)} %collective-permute-done.1.refs_1_) | copy-start | bytes 147460
  53.6 1.8 %copy-start.6 = (bf16[6,32,128]{2,1,0:T(8,128)(2,1)}, bf16[6,32,128]{2,1,0:T(8,128)(2,1)S(1)}, u32[]{:S(2)}) copy-start(bf16[6,32,128]{2,1,0:T(8,128)(2,1)S(1)} %collective-permute-done.2.refs_2_) | copy-start | bytes 147460
  55.4 0.6 copy-start.7
  61.7 11.6 %all-to-all-start.1 = ((bf16[8,64,384]{2,1,0:T(8,128)(2,1)}), bf16[8,64,384]{2,1,0:T(8,128)(2,1)S(1)}, u32[]{:S(2)}, u32[]{:S(2)}) async-start(bf16[8,64,384]{2,1,0:T(8,128)(2,1)} %get-tuple-element.20), calls=%async_computation.1 | async-start | bytes 786432 | tf_op jit(solution)/shard_map/all_to_all | solution.py:20
  66.4 0.9 copy-start.2
  67.4 10.7 %collective-permute-start.4 = (bf16[256,384]{1,0:T(8,128)(2,1)S(1)}, bf16[256,384]{1,0:T(8,128)(2,1)S(1)}, u32[]{:S(2)}, u32[]{:S(2)}) collective-permute-start(bf16[256,384]{1,0:T(8,128)(2,1)S(1)} %dynamic-slice_convert_fusion), channel_id=1, source_target_pairs={{0,1},{1,0},{2,3},{3,2},{4,5},{5,4},{6,7},{7,6},{8,9},{9,8},{10,11... | collective-permute-start | bytes 589832 | tf_op jit(solution)/shard_map/ppermute | solution.py:157

commit v3 on v1

v3 whole, which is shorter than its diff:
```python
import math

import jax
import jax.numpy as jnp
from jax import lax
from jax.experimental import pallas as pl
from jax.experimental.pallas import tpu as pltpu
from jax.sharding import PartitionSpec as P

F32 = jnp.float32
BF16 = jnp.bfloat16
NEAR = 4
PAIR = 2
PARTS = 6
SMALL, LARGE = 12 << 20, 58 << 20


def exchange(tiles, axis, groups=None):
    return lax.all_to_all(tiles, axis, 0, 0, tiled=True, axis_index_groups=groups)


def swapped(value, axis, pairs):
    return lax.ppermute(value, axis, [(a, b) for a, b in pairs] + [(b, a) for a, b in pairs])


def space_pairings(count):
    far_odd = [(p, p + 2) for p in range(count - 2) if p % 4 >= 2]
    far_even = [(p, p + 2) for p in range(count - 2) if p % 4 < 2]
    near_odd = [(p, p + 1) for p in range(1, count - 1, 2)]
    near_even = [(p, p + 1) for p in range(0, count - 1, 2)]
    return far_odd, near_odd, far_even, near_even


def lists_of_pairings(place):
    far, near = lax.rem(place, 4) >= 2, lax.rem(place, 2) == 1
    for up, below, above in ((far, 0, 3), (near, 1, 2), (~far, 0, 3), (~near, 1, 2)):
        yield jnp.where(up, below, above), jnp.where(up, above, below)


def vmem():
    return pl.BlockSpec(memory_space=pltpu.VMEM)


def smem():
    return pl.BlockSpec(memory_space=pltpu.SMEM)


def limit(size):
    return pltpu.CompilerParams(vmem_limit_bytes=size)


def split_kernel(side_ref, tiles_ref, own_ref, other_ref):
    share = own_ref.shape[0]

    def summed(start):
        rows = pl.ds(pl.multiple_of(start, share), share)
        total = tiles_ref[0, rows].astype(F32)
        for j in range(1, tiles_ref.shape[0]):
            total = total + tiles_ref[j, rows].astype(F32)
        return total

    other_ref[...] = summed((1 - side_ref[0]) * share).astype(BF16)
    own_ref[...] = summed(side_ref[0] * share)


def summed_halves(side, tiles):
    _, rows, unknowns = tiles.shape
    share = rows // PAIR
    return pl.pallas_call(
        split_kernel,
        out_shape=[
            jax.ShapeDtypeStruct((share, unknowns), F32),
            jax.ShapeDtypeStruct((share, unknowns), BF16),
        ],
        in_specs=[smem(), vmem()],
        out_specs=[vmem(), vmem()],
        compiler_params=limit(SMALL),
    )(side, tiles)


def pick_kernel(place_ref, send_ref, own_ref, arrived_ref, primal_ref, *out_refs):
    primal_ref[...] = (own_ref[...] + arrived_ref[...].astype(F32)).astype(BF16)
    size = out_refs[0].shape[2]
    for (sent, _), out_ref in zip(lists_of_pairings(place_ref[0]), out_refs):
        for t in range(out_ref.shape[0]):
            start = pl.multiple_of(send_ref[sent, t] * size, size)
            out_ref[t] = primal_ref[:, pl.ds(start, size)]


def sum_and_pick(place, lists, own, arrived, size):
    share, unknowns = own.shape
    count, length = lists.shape
    return pl.pallas_call(
        pick_kernel,
        out_shape=[jax.ShapeDtypeStruct((share, unknowns), BF16)]
        + [jax.ShapeDtypeStruct((length, share, size), BF16)] * count,
        in_specs=[smem(), smem(), vmem(), vmem()],
        out_specs=[vmem()] * (1 + count),
        compiler_params=limit(SMALL),
    )(place, lists, own, arrived)


def bring_kernel(_, op_hbm, op_ref, sems):
    part = op_hbm.shape[0] // PARTS
    copies = []
    for i in range(PARTS):
        cut = pl.ds(i * part, part)
        copies.append(pltpu.make_async_copy(op_hbm.at[cut], op_ref.at[cut], sems.at[i]))
        copies[-1].start()
    for copy in copies:
        copy.wait()


def brought_in(after, op_blocks):
    hbm = pl.BlockSpec(memory_space=pltpu.HBM)
    return pl.pallas_call(
        bring_kernel,
        out_shape=pltpu.VMEM(op_blocks.shape, BF16),
        in_specs=[hbm, hbm],
        out_specs=vmem(),
        scratch_shapes=[pltpu.SemaphoreType.DMA((PARTS,))],
        compiler_params=limit(LARGE),
    )(after, op_blocks)


def apply_kernel(place_ref, side_ref, counts_ref, cols_ref, primal_ref, *refs):
    *ghost_refs, op_ref, applied_ref, mine_ref, other_ref, held, halves = refs
    rows, slots, size, _ = op_ref.shape
    share = primal_ref.shape[0]
    half = mine_ref.shape[1]
    per = half // size
    for b in range(rows):
        held[b] = primal_ref[:, b * size : (b + 1) * size]
    for (_, received), ghost_ref in zip(lists_of_pairings(place_ref[0]), ghost_refs):
        length = ghost_ref.shape[0]
        held[pl.ds(rows + received * length, length)] = ghost_ref[...]
    for r in range(rows):
        blocks = []
        for k in range(slots):
            block = held[cols_ref[r, k]]
            blocks.append(jnp.where(k < counts_ref[r], block, jnp.zeros_like(block)))
        out = lax.dot_general(
            jnp.concatenate(blocks, axis=1),
            jnp.concatenate([op_ref[r, k] for k in range(slots)], axis=1),
            (((1,), (1,)), ((), ())),
            preferred_element_type=F32,
        ).astype(BF16)
        applied_ref[:, r * size : (r + 1) * size] = out
        halves[r // per, :, (r % per) * size : (r % per + 1) * size] = out
    for ref, h in ((other_ref, 1 - side_ref[0]), (mine_ref, side_ref[0])):
        ref[:share] = halves[h]
        ref[share:] = primal_ref[:, pl.ds(pl.multiple_of(h * half, half), half)]


def applied_and_halves(place, side, counts, cols, primal, ghosts, op_blocks):
    share, unknowns = primal.shape
    rows, slots, size, _ = op_blocks.shape
    held = rows + sum(g.shape[0] for g in ghosts)
    half = jax.ShapeDtypeStruct((2 * share, unknowns // PAIR), BF16)
    return pl.pallas_call(
        apply_kernel,
        out_shape=[jax.ShapeDtypeStruct((share, unknowns), BF16), half, half],
        in_specs=[smem()] * 4 + [vmem()] * (2 + len(ghosts)),
        out_specs=[vmem()] * 3,
        scratch_shapes=[
            pltpu.VMEM((held, share, size), BF16),
            pltpu.VMEM((PAIR, share, unknowns // PAIR), BF16),
        ],
        compiler_params=limit(SMALL),
    )(place, side, counts, cols, primal, *ghosts, op_blocks)


def per_device(
    snaps_primal, snaps_adjoint, coef_primal, coef_adjoint, op_blocks, counts, col_index, ghost_send
):
    ways, space = lax.axis_size("snap"), lax.axis_size("space")
    runs = ways // PAIR
    modes = coef_primal.shape[1]
    share = modes // ways
    unknowns = snaps_primal.shape[1]
    half = unknowns // PAIR
    size = op_blocks.shape[2]
    side = lax.axis_index("snap") % PAIR
    along_x = [[x * PAIR + y for x in range(runs)] for y in range(PAIR)]
    pair = [(x * PAIR, x * PAIR + 1) for x in range(runs)]
    deep = space // 2
    along_z = [[h * deep + z * 2 + c for z in range(deep // 2)] for h in range(2) for c in range(2)]
    across_z = [[h * deep + z * 2 + c for h in range(2) for c in range(2)] for z in range(deep // 2)]
    around = [
        [p * ways + x * PAIR + y for y in range(PAIR) for p in group]
        for group in across_z
        for x in range(runs)
    ]
    sides = side.reshape(1).astype(jnp.int32)
    place = lax.axis_index("space").reshape(1).astype(jnp.int32)

    primal_part = jnp.einsum("mr,ms->rs", coef_primal, snaps_primal, preferred_element_type=F32)
    primal_part, snaps_adjoint = lax.optimization_barrier((primal_part.astype(BF16), snaps_adjoint))
    primal_tiles = primal_part.reshape(runs, PAIR * share, unknowns)
    primal_tiles = exchange(primal_tiles, "snap", along_x)

    adjoint_part = jnp.einsum("mr,ms->rs", coef_adjoint, snaps_adjoint, preferred_element_type=F32)
    adjoint_part = adjoint_part.astype(BF16)
    adjoint_own = lax.dynamic_slice_in_dim(adjoint_part, side * half, half, axis=1)
    adjoint_other = lax.dynamic_slice_in_dim(adjoint_part, (1 - side) * half, half, axis=1)
    adjoint_other = swapped(adjoint_other, "snap", pair)

    own, other = summed_halves(sides, primal_tiles)
    adjoint = (adjoint_own.astype(F32) + adjoint_other.astype(F32)).astype(BF16)
    _, adjoint = lax.optimization_barrier((other, adjoint))
    arrived = swapped(other, "snap", pair)
    adjoint = exchange(adjoint.reshape(runs, modes // runs, half), "snap", along_x)
    adjoint = adjoint.astype(F32).sum(axis=0).astype(BF16)

    primal, *outgoing = sum_and_pick(place, ghost_send[0], own, arrived, size)
    ghosts = [swapped(o, "space", w) for o, w in zip(outgoing, space_pairings(space))]
    op_near = brought_in(outgoing[-1], op_blocks)
    *ghosts, adjoint = lax.optimization_barrier((*ghosts, adjoint))
    adjoint = exchange(jnp.broadcast_to(adjoint[None], (runs, *adjoint.shape)), "snap", along_x)
    adjoint = adjoint.reshape(modes, half)
    applied, mine, other = applied_and_halves(place, sides, counts, col_index, primal, ghosts, op_near)
    arrived = swapped(other, "snap", pair)

    def product(rows):
        return jnp.einsum("as,bs->ab", rows, adjoint, preferred_element_type=F32).astype(BF16)

    here, there = product(mine), product(arrived)
    first = side == 0
    products = jnp.stack([jnp.where(first, here, there), jnp.where(first, there, here)])
    rows = 2 * share // NEAR
    tiles = exchange(products.reshape(PAIR * NEAR, rows, modes), ("space", "snap"), around)
    total = tiles.astype(F32).sum(axis=0).astype(BF16)
    every = exchange(jnp.broadcast_to(total[None], (deep // 2, rows, modes)), "space", along_z)
    total = every.astype(F32).sum(axis=0) * (1.0 / math.sqrt(unknowns * space))
    total = exchange(jnp.broadcast_to(total[None], (NEAR, rows, modes)), "space", across_z)
    total = total.reshape(2 * share, modes)
    return (primal, applied, total[:share].T, total[share:].T)


def solution(mesh):
    placed = (
        P("snap", "space"),
        P("snap", "space"),
        P("snap", None),
        P("snap", None),
        P("space", None, None, None),
        P("space"),
        P("space", None),
        P("space", None, None),
    )
    return jax.shard_map(
        per_device,
        mesh=mesh,
        in_specs=placed,
        out_specs=(P("snap", "space"), P("snap", "space"), P(None, "snap"), P(None, "snap")),
        check_vma=False,
    )
```

time: 146 us -> 140 us (0.959)
  Pallas kernels: 0 us -> 8.04 us
  local copies, waits for them, and re-layouts: 14.6 us -> 7.53 us
  other arithmetic: 7.77 us -> 3.55 us
  blocking collectives: 48.8 us -> 46.4 us
  starting transfers between devices: 37.9 us -> 40.2 us
  matrix products: 10.9 us -> 8.88 us
    all_to_all x4 -> x3, waiting for transfers between devices: 23.9 us -> 5.24 us  [exchange(): lax.all_to_all(tiles, axis, 0, 0, tiled=True, axis_index_groups=groups)]
    ppermute x4 -> x7, waiting for transfers between devices: 0.13 us -> 18.2 us  [swapped(): lax.ppermute(value, axis, [(a, b) for a, b in pairs] + [(b, a) for a, b i...]
    ppermute x4 -> x7, starting transfers between devices: 16.4 us -> 27.2 us  [swapped(): lax.ppermute(value, axis, [(a, b) for a, b in pairs] + [(b, a) for a, b i...]
    all_to_all x4 -> x3, starting transfers between devices: 21.5 us -> 13 us  [exchange(): lax.all_to_all(tiles, axis, 0, 0, tiled=True, axis_index_groups=groups)]
    pallas_call x0 -> x4, Pallas kernels: none -> 8.04 us  [the longest x1 2.98 us: applied_and_halves(): pl.pallas_call(apply_kernel, out_shape=[jax.ShapeDtypeStruct((share, unkn...]
    reshape x4 -> x0, local copies, waits for them, and re-layouts: 4.13 us -> none  [the longest x1 2.61 us: per_device(): snaps_adjoint.reshape(-1, ways, piece)]
    gather x2 -> x0, local copies, waits for them, and re-layouts: 2.91 us -> none  [the longest x1 1.66 us: per_device(): picked = jnp.take(extended, col_index, axis=1)]
    all_to_all x3, blocking collectives: 48.8 us -> 46.4 us  [exchange(): lax.all_to_all(tiles, axis, 0, 0, tiled=True, axis_index_groups=groups)]
  transfers between devices with their start and end apart: 8 -> 10, of which waited for: 4 -> 4; matrix products, arithmetic and copies ran while one was open for 17% -> 3% of each run, Pallas kernels for 0% -> 5%
where the time goes in v3:
time: 140 us; the launch traced here: 139 us
  blocking collectives  46.4 us (33%)
  starting transfers between devices  40.2 us (29%)
  waiting for transfers between devices  23.4 us (17%)
  matrix products  8.88 us (6%)
  Pallas kernels  8.04 us (6%)
  local copies, waits for them, and re-layouts  7.53 us (5%)
  other arithmetic  3.55 us (3%)
    all_to_all x3, blocking collectives, exchange(): lax.all_to_all(tiles, axis, 0, 0, tiled=True, axis_index_groups=groups)  46.4 us
    ppermute x7, starting transfers between devices, swapped(): lax.ppermute(value, axis, [(a, b) for a, b in pairs] + [(b, a) for a, b i...  27.2 us
    ppermute x7, waiting for transfers between devices, swapped(): lax.ppermute(value, axis, [(a, b) for a, b in pairs] + [(b, a) for a, b i...  18.2 us
    all_to_all x3, starting transfers between devices, exchange(): lax.all_to_all(tiles, axis, 0, 0, tiled=True, axis_index_groups=groups)  13 us
    all_to_all x3, waiting for transfers between devices, exchange(): lax.all_to_all(tiles, axis, 0, 0, tiled=True, axis_index_groups=groups)  5.24 us
    dot_general x1, matrix products, per_device(): jnp.einsum('mr,ms->rs', coef_adjoint, snaps_adjoint, preferred_element_ty...  3.19 us
    pallas_call x1, Pallas kernels, applied_and_halves(): pl.pallas_call(apply_kernel, out_shape=[jax.ShapeDtypeStruct((share, unkn...  2.98 us
    dot_general x2, matrix products, product(): jnp.einsum('as,bs->ab', rows, adjoint, preferred_element_type=F32)  2.97 us
  transfers between devices with their start and end apart: 10, of which 4 were waited for; matrix products, arithmetic and copies ran while one was open for 3% of the time, Pallas kernels for 5%

profile of v3, /device:TPU:1, one launch (start us, length us, event | category | flops | bytes accessed | tf_op | source)
XLA Modules:
  0.0 139.0 jit_solution(3403743099757454743)
XLA Ops:
  2.0 2.7 %convolution_convert_fusion.1 = bf16[256,3072]{1,0:T(8,128)(2,1)} fusion(bf16[256,256]{1,0:T(8,128)(2,1)} %param.10, bf16[256,3072]{1,0:T(8,128)(2,1)S(1)} %copy-done), kind=kOutput, calls=%fused_computation.1 | convolution fusion | flops 403439616 | bytes 3276800 | tf_op jit(solution)/shard_map/mr,ms->rs/dot_general | solution.py:197
  4.8 3.2 %convolution_convert_fusion = bf16[3072,256]{1,0:T(8,128)(2,1)} fusion(bf16[256,3072]{1,0:T(8,128)(2,1)} %param.9, bf16[256,256]{1,0:T(8,128)(2,1)S(1)} %copy-done.5), kind=kOutput, calls=%fused_computation | convolution fusion | flops 403439616 | bytes 3276800 | tf_op jit(solution)/shard_map/mr,ms->rs/dot_general | solution.py:202
  8.0 2.1 %dynamic-slice_bitcast_fusion = bf16[256,1536]{0,1:T(8,128)(2,1)} fusion(bf16[3072,256]{1,0:T(8,128)(2,1)} %convolution_convert_fusion, s32[]{:T(128)S(6)} %select_n.27), kind=kLoop, calls=%fused_computation.6 | loop fusion | bytes 1572868 | tf_op jit(solution)/shard_map/dynamic_slice | solution.py:205
  10.0 4.0 %collective-permute-start.5 = (bf16[256,1536]{0,1:T(8,128)(2,1)}, bf16[256,1536]{0,1:T(8,128)(2,1)S(1)}, u32[]{:S(2)}, u32[]{:S(2)}) collective-permute-start(bf16[256,1536]{0,1:T(8,128)(2,1)} %dynamic-slice_bitcast_fusion), channel_id=1, source_target_pairs={{0,1},{2,3},{4,5},{6,7},{1,0},{3,2},{5,4},{7,6},{8,9},{10,11},{12,... | collective-permute-start | bytes 2359304 | tf_op jit(solution)/shard_map/ppermute | solution.py:23
  14.1 4.4 %all-to-all-start = ((bf16[4,64,3072]{2,1,0:T(8,128)(2,1)}), bf16[4,64,3072]{2,1,0:T(8,128)(2,1)}, u32[]{:S(2)}, u32[]{:S(2)}) async-start(bf16[4,64,3072]{2,1,0:T(8,128)(2,1)} %bitcast.32), calls=%async_computation | async-start | bytes 3145728 | tf_op jit(solution)/shard_map/all_to_all | solution.py:19
  18.5 8.3 %collective-permute-done.5 = bf16[256,1536]{0,1:T(8,128)(2,1)S(1)} collective-permute-done((bf16[256,1536]{0,1:T(8,128)(2,1)}, bf16[256,1536]{0,1:T(8,128)(2,1)S(1)}, u32[]{:S(2)}, u32[]{:S(2)}) %collective-permute-start.5) | collective-permute-done | bytes 786464 | tf_op jit(solution)/shard_map/ppermute | solution.py:23
  26.7 2.2 %fusion = bf16[256,1536]{0,1:T(8,128)(2,1)} fusion(bf16[256,1536]{0,1:T(8,128)(2,1)S(1)} %collective-permute-done.5, bf16[3072,256]{1,0:T(8,128)(2,1)} %convolution_convert_fusion, s32[]{:T(128)S(6)} %select_n.26), kind=kLoop, calls=%fused_computation.3 | loop fusion | flops 1572864 | bytes 2359300 | tf_op jit(solution)/shard_map/convert_element_type | solution.py:209
  28.9 5.2 %all-to-all-done.tiles_ref = bf16[4,64,3072]{2,1,0:T(8,128)(2,1)} async-done(((bf16[4,64,3072]{2,1,0:T(8,128)(2,1)}), bf16[4,64,3072]{2,1,0:T(8,128)(2,1)}, u32[]{:S(2)}, u32[]{:S(2)}) %all-to-all-start) | async-done | bytes 1572896 | tf_op jit(solution)/shard_map/all_to_all | solution.py:19
  34.2 1.6 %shard_map.111 = (f32[32,3072]{1,0:T(8,128)S(1)}, bf16[32,3072]{1,0:T(8,128)(2,1)S(1)}) custom-call(s32[1]{0:T(128)} %bitcast.2.side_ref, bf16[4,64,3072]{2,1,0:T(8,128)(2,1)} %all-to-all-done.tiles_ref), custom_call_target="tpu_custom_call" | custom-call | tf_op jit(solution)/shard_map/pallas_call | solution.py:69
  35.8 2.3 %copy.15 = bf16[256,1536]{1,0:T(8,128)(2,1)} copy(bf16[256,1536]{0,1:T(8,128)(2,1)} %fusion) | data formatting | bytes 1572864 | tf_op jit(solution)/shard_map/optimization_barrier | solution.py:210
  38.1 4.2 %all-to-all-start.1 = ((bf16[4,64,1536]{2,1,0:T(8,128)(2,1)}), bf16[4,64,1536]{2,1,0:T(8,128)(2,1)}, u32[]{:S(2)}, u32[]{:S(2)}) async-start(bf16[4,64,1536]{2,1,0:T(8,128)(2,1)} %bitcast.33), calls=%async_computation.1 | async-start | bytes 1572864 | tf_op jit(solution)/shard_map/all_to_all | solution.py:19
  42.3 2.5 %collective-permute-start = (bf16[32,3072]{1,0:T(8,128)(2,1)S(1)}, bf16[32,3072]{1,0:T(8,128)(2,1)S(1)}, u32[]{:S(2)}, u32[]{:S(2)}) collective-permute-start(bf16[32,3072]{1,0:T(8,128)(2,1)S(1)} %get-tuple-element.24), channel_id=1, source_target_pairs={{0,1},{2,3},{4,5},{6,7},{1,0},{3,2},{5,4},{7,6},{8,9},{10,11},{12,... | collective-permute-start | bytes 589832 | tf_op jit(solution)/shard_map/ppermute | solution.py:23
  44.9 3.9 %collective-permute-done.arrived_ref = bf16[32,3072]{1,0:T(8,128)(2,1)S(1)} collective-permute-done((bf16[32,3072]{1,0:T(8,128)(2,1)S(1)}, bf16[32,3072]{1,0:T(8,128)(2,1)S(1)}, u32[]{:S(2)}, u32[]{:S(2)}) %collective-permute-start) | collective-permute-done | bytes 196640 | tf_op jit(solution)/shard_map/ppermute | solution.py:23
  50.7 13.7 %collective-permute-start.2 = (bf16[6,32,128]{2,1,0:T(8,128)(2,1)S(1)}, bf16[6,32,128]{2,1,0:T(8,128)(2,1)S(1)}, u32[]{:S(2)}, u32[]{:S(2)}) collective-permute-start(bf16[6,32,128]{2,1,0:T(8,128)(2,1)S(1)} %get-tuple-element.27), channel_id=1, source_target_pairs={{8,16},{24,32},{40,48},{56,64},{72,80},{88,96},{104,112},{120,128}... | collective-permute-start | bytes 147464 | tf_op jit(solution)/shard_map/ppermute | solution.py:23
  64.4 1.9 %collective-permute-start.3 = (bf16[6,32,128]{2,1,0:T(8,128)(2,1)S(1)}, bf16[6,32,128]{2,1,0:T(8,128)(2,1)S(1)}, u32[]{:S(2)}, u32[]{:S(2)}) collective-permute-start(bf16[6,32,128]{2,1,0:T(8,128)(2,1)S(1)} %get-tuple-element.28), channel_id=1, source_target_pairs={{0,16},{8,24},{32,48},{40,56},{64,80},{72,88},{96,112},{104,120},{... | collective-permute-start | bytes 147464 | tf_op jit(solution)/shard_map/ppermute | solution.py:23
  66.4 2.3 %collective-permute-start.4 = (bf16[6,32,128]{2,1,0:T(8,128)(2,1)S(1)}, bf16[6,32,128]{2,1,0:T(8,128)(2,1)S(1)}, u32[]{:S(2)}, u32[]{:S(2)}) collective-permute-start(bf16[6,32,128]{2,1,0:T(8,128)(2,1)S(1)} %get-tuple-element.29._), channel_id=1, source_target_pairs={{0,8},{16,24},{32,40},{48,56},{64,72},{80,88},{96,104},{112,120},{... | collective-permute-start | bytes 147464 | tf_op jit(solution)/shard_map/ppermute | solution.py:23
  71.0 4.5 %all-to-all-start.2 = ((bf16[4,64,1536]{2,1,0:T(8,128)(2,1)}), bf16[4,64,1536]{2,1,0:T(8,128)(2,1)}, u32[]{:S(2)}, u32[]{:S(2)}) async-start(bf16[4,64,1536]{2,1,0:T(8,128)(2,1)} %broadcast_in_dim.6), calls=%async_computation.2 | async-start | bytes 1572864 | tf_op jit(solution)/shard_map/all_to_all | solution.py:19
  75.5 2.2 %shard_map.113.refs_4_ = bf16[24,5,128,128]{3,2,1,0:T(8,128)(2,1)S(1)} custom-call(bf16[6,32,128]{2,1,0:T(8,128)(2,1)} %copy-done.2, bf16[24,5,128,128]{3,2,1,0:T(8,128)(2,1)} %op_hbm.1), custom_call_target="tpu_custom_call" | custom-call | tf_op jit(solution)/shard_map/pallas_call | solution.py:116
  77.7 3.0 %shard_map.114 = (bf16[32,3072]{1,0:T(8,128)(2,1)}, bf16[64,1536]{1,0:T(8,128)(2,1)S(1)}, bf16[64,1536]{1,0:T(8,128)(2,1)}) custom-call(s32[1]{0:T(128)} %bitcast.place_ref, s32[1]{0:T(128)} %bitcast.2.side_ref, s32[24]{0:T(128)S(1)} %copy-done.4, s32[24,5]{1,0:T(8,128)S(1)} %copy.16.cols_ref, bf16[32,3072]{1,0:T(8,128)(2,1)S(1)} %copy-done.1, ...), custom_call_target="tpu_custom_call" | custom-call | tf_op jit(solution)/shard_map/pallas_call | solution.py:160
  80.7 2.1 %collective-permute-start.6 = (bf16[64,1536]{1,0:T(8,128)(2,1)}, bf16[64,1536]{1,0:T(8,128)(2,1)S(1)}, u32[]{:S(2)}, u32[]{:S(2)}) collective-permute-start(bf16[64,1536]{1,0:T(8,128)(2,1)} %get-tuple-element.39), channel_id=1, source_target_pairs={{0,1},{2,3},{4,5},{6,7},{1,0},{3,2},{5,4},{7,6},{8,9},{10,11},{12,... | collective-permute-start | bytes 589832 | tf_op jit(solution)/shard_map/ppermute | solution.py:23
  82.8 6.1 %collective-permute-done.6 = bf16[64,1536]{1,0:T(8,128)(2,1)S(1)} collective-permute-done((bf16[64,1536]{1,0:T(8,128)(2,1)}, bf16[64,1536]{1,0:T(8,128)(2,1)S(1)}, u32[]{:S(2)}, u32[]{:S(2)}) %collective-permute-start.6) | collective-permute-done | bytes 196640 | tf_op jit(solution)/shard_map/ppermute | solution.py:23
  91.9 16.2 %all_to_all.30 = bf16[8,16,256]{2,1,0:T(8,128)(2,1)S(1)} all-to-all(bf16[8,16,256]{2,1,0:T(8,128)(2,1)S(1)} %bitcast.34), channel_id=1, replica_groups={{0,8,256,264,1,9,257,265},{2,10,258,266,3,11,259,267},{4,12,260,268,5,1..., dimensions={0} | all-to-all | bytes 131072 | tf_op jit(solution)/shard_map/all_to_all | solution.py:19
  108.1 19.3 %all_to_all.31 = bf16[16,16,256]{2,1,0:T(8,128)(2,1)S(1)} all-to-all(bf16[16,16,256]{2,1,0:T(8,128)(2,1)S(1)} %broadcast_in_dim.7), channel_id=1, replica_groups={{0,16,32,48,64,80,96,112,128,144,160,176,192,208,224,240},{8,24,40,56,7..., dimensions={0} | all-to-all | bytes 262144 | tf_op jit(solution)/shard_map/all_to_all | solution.py:19
  127.4 10.9 %all_to_all.32 = f32[4,16,256]{2,1,0:T(8,128)S(1)} all-to-all(f32[4,16,256]{2,1,0:T(8,128)S(1)} %broadcast_in_dim.8), channel_id=1, replica_groups={{0,8,256,264},{16,24,272,280},{32,40,288,296},{48,56,304,312},{64,72,32..., dimensions={0} | all-to-all | bytes 131072 | tf_op jit(solution)/shard_map/all_to_all | solution.py:19
  (34 shorter events, 9.4 us)
Async XLA Ops:
  0.6 1.4 %copy-start = (bf16[256,3072]{1,0:T(8,128)(2,1)S(1)}, bf16[256,3072]{1,0:T(8,128)(2,1)}, u32[]{:S(2)}) copy-start(bf16[256,3072]{1,0:T(8,128)(2,1)} %param.8) | copy-start | bytes 4718596
  2.0 2.7 %copy-start.5 = (bf16[256,256]{1,0:T(8,128)(2,1)S(1)}, bf16[256,256]{1,0:T(8,128)(2,1)}, u32[]{:S(2)}) copy-start(bf16[256,256]{1,0:T(8,128)(2,1)} %param.11) | copy-start | bytes 393220
  10.0 16.7 %collective-permute-start.5 = (bf16[256,1536]{0,1:T(8,128)(2,1)}, bf16[256,1536]{0,1:T(8,128)(2,1)S(1)}, u32[]{:S(2)}, u32[]{:S(2)}) collective-permute-start(bf16[256,1536]{0,1:T(8,128)(2,1)} %dynamic-slice_bitcast_fusion), channel_id=1, source_target_pairs={{0,1},{2,3},{4,5},{6,7},{1,0},{3,2},{5,4},{7,6},{8,9},{10,11},{12,... | collective-permute-start | bytes 2359304 | tf_op jit(solution)/shard_map/ppermute | solution.py:23
  14.1 20.1 %all-to-all-start = ((bf16[4,64,3072]{2,1,0:T(8,128)(2,1)}), bf16[4,64,3072]{2,1,0:T(8,128)(2,1)}, u32[]{:S(2)}, u32[]{:S(2)}) async-start(bf16[4,64,3072]{2,1,0:T(8,128)(2,1)} %bitcast.32), calls=%async_computation | async-start | bytes 3145728 | tf_op jit(solution)/shard_map/all_to_all | solution.py:19
  35.8 13.0 %copy-start.3 = (s32[1,4,6]{2,1,0:T(4,128)S(1)}, s32[1,4,6]{2,1,0:T(4,128)}, u32[]{:S(2)}) copy-start(s32[1,4,6]{2,1,0:T(4,128)} %param.15) | copy-start | bytes 292
  38.1 30.6 %all-to-all-start.1 = ((bf16[4,64,1536]{2,1,0:T(8,128)(2,1)}), bf16[4,64,1536]{2,1,0:T(8,128)(2,1)}, u32[]{:S(2)}, u32[]{:S(2)}) async-start(bf16[4,64,1536]{2,1,0:T(8,128)(2,1)} %bitcast.33), calls=%async_computation.1 | async-start | bytes 1572864 | tf_op jit(solution)/shard_map/all_to_all | solution.py:19
  42.3 6.4 %collective-permute-start = (bf16[32,3072]{1,0:T(8,128)(2,1)S(1)}, bf16[32,3072]{1,0:T(8,128)(2,1)S(1)}, u32[]{:S(2)}, u32[]{:S(2)}) collective-permute-start(bf16[32,3072]{1,0:T(8,128)(2,1)S(1)} %get-tuple-element.24), channel_id=1, source_target_pairs={{0,1},{2,3},{4,5},{6,7},{1,0},{3,2},{5,4},{7,6},{8,9},{10,11},{12,... | collective-permute-start | bytes 589832 | tf_op jit(solution)/shard_map/ppermute | solution.py:23
  50.0 20.9 %copy-start.2 = (bf16[6,32,128]{2,1,0:T(8,128)(2,1)}, bf16[6,32,128]{2,1,0:T(8,128)(2,1)S(1)}, u32[]{:S(2)}) copy-start(bf16[6,32,128]{2,1,0:T(8,128)(2,1)S(1)} %get-tuple-element.29._) | copy-start | bytes 147460
  50.0 19.9 %collective-permute-start.1 = (bf16[6,32,128]{2,1,0:T(8,128)(2,1)S(1)}, bf16[6,32,128]{2,1,0:T(8,128)(2,1)S(1)}, u32[]{:S(2)}, u32[]{:S(2)}) collective-permute-start(bf16[6,32,128]{2,1,0:T(8,128)(2,1)S(1)} %get-tuple-element.26), channel_id=1, source_target_pairs={{16,32},{24,40},{48,64},{56,72},{80,96},{88,104},{112,128},{120,13... | collective-permute-start | bytes 147464 | tf_op jit(solution)/shard_map/ppermute | solution.py:23
  50.7 19.3 %collective-permute-start.2 = (bf16[6,32,128]{2,1,0:T(8,128)(2,1)S(1)}, bf16[6,32,128]{2,1,0:T(8,128)(2,1)S(1)}, u32[]{:S(2)}, u32[]{:S(2)}) collective-permute-start(bf16[6,32,128]{2,1,0:T(8,128)(2,1)S(1)} %get-tuple-element.27), channel_id=1, source_target_pairs={{8,16},{24,32},{40,48},{56,64},{72,80},{88,96},{104,112},{120,128}... | collective-permute-start | bytes 147464 | tf_op jit(solution)/shard_map/ppermute | solution.py:23
  64.4 5.6 %collective-permute-start.3 = (bf16[6,32,128]{2,1,0:T(8,128)(2,1)S(1)}, bf16[6,32,128]{2,1,0:T(8,128)(2,1)S(1)}, u32[]{:S(2)}, u32[]{:S(2)}) collective-permute-start(bf16[6,32,128]{2,1,0:T(8,128)(2,1)S(1)} %get-tuple-element.28), channel_id=1, source_target_pairs={{0,16},{8,24},{32,48},{40,56},{64,80},{72,88},{96,112},{104,120},{... | collective-permute-start | bytes 147464 | tf_op jit(solution)/shard_map/ppermute | solution.py:23
  66.4 9.1 %copy-start.6 = (s32[24,5]{0,1:T(8,128)S(1)}, s32[24,5]{0,1:T(8,128)}, u32[]{:S(2)}) copy-start(s32[24,5]{0,1:T(8,128)} %param.14) | copy-start | bytes 1444
  66.4 3.6 %collective-permute-start.4 = (bf16[6,32,128]{2,1,0:T(8,128)(2,1)S(1)}, bf16[6,32,128]{2,1,0:T(8,128)(2,1)S(1)}, u32[]{:S(2)}, u32[]{:S(2)}) collective-permute-start(bf16[6,32,128]{2,1,0:T(8,128)(2,1)S(1)} %get-tuple-element.29._), channel_id=1, source_target_pairs={{0,8},{16,24},{32,40},{48,56},{64,72},{80,88},{96,104},{112,120},{... | collective-permute-start | bytes 147464 | tf_op jit(solution)/shard_map/ppermute | solution.py:23
  71.0 17.9 %all-to-all-start.2 = ((bf16[4,64,1536]{2,1,0:T(8,128)(2,1)}), bf16[4,64,1536]{2,1,0:T(8,128)(2,1)}, u32[]{:S(2)}, u32[]{:S(2)}) async-start(bf16[4,64,1536]{2,1,0:T(8,128)(2,1)} %broadcast_in_dim.6), calls=%async_computation.2 | async-start | bytes 1572864 | tf_op jit(solution)/shard_map/all_to_all | solution.py:19
  75.5 2.2 %copy-start.1 = (bf16[32,3072]{1,0:T(8,128)(2,1)S(1)}, bf16[32,3072]{1,0:T(8,128)(2,1)}, u32[]{:S(2)}) copy-start(bf16[32,3072]{1,0:T(8,128)(2,1)} %get-tuple-element.18.primal_ref) | copy-start | bytes 589828
  75.5 2.2 %copy-start.4 = (s32[24]{0:T(128)S(1)}, s32[24]{0:T(128)}, u32[]{:S(2)}) copy-start(s32[24]{0:T(128)} %counts_ref.1) | copy-start | bytes 292
  80.7 8.1 %collective-permute-start.6 = (bf16[64,1536]{1,0:T(8,128)(2,1)}, bf16[64,1536]{1,0:T(8,128)(2,1)S(1)}, u32[]{:S(2)}, u32[]{:S(2)}) collective-permute-start(bf16[64,1536]{1,0:T(8,128)(2,1)} %get-tuple-element.39), channel_id=1, source_target_pairs={{0,1},{2,3},{4,5},{6,7},{1,0},{3,2},{5,4},{7,6},{8,9},{10,11},{12,... | collective-permute-start | bytes 589832 | tf_op jit(solution)/shard_map/ppermute | solution.py:23

commit v4 on v2

v4 whole, which is shorter than its diff:
```python
import math

import jax
import jax.numpy as jnp
from jax import lax
from jax.experimental import pallas as pl
from jax.experimental.pallas import tpu as pltpu
from jax.sharding import PartitionSpec as P

F32 = jnp.float32
BF16 = jnp.bfloat16
NEAR = 4
PARTS = 6
SMALL, LARGE = 12 << 20, 58 << 20


def exchange(tiles, axis, groups=None):
    return lax.all_to_all(tiles, axis, 0, 0, tiled=True, axis_index_groups=groups)


def swapped(value, axis, pairs):
    return lax.ppermute(value, axis, [(a, b) for a, b in pairs] + [(b, a) for a, b in pairs])


def space_pairings(count):
    far_odd = [(p, p + 2) for p in range(count - 2) if p % 4 >= 2]
    far_even = [(p, p + 2) for p in range(count - 2) if p % 4 < 2]
    near_odd = [(p, p + 1) for p in range(1, count - 1, 2)]
    near_even = [(p, p + 1) for p in range(0, count - 1, 2)]
    return far_odd, near_odd, far_even, near_even


def lists_of_pairings(place):
    far, near = lax.rem(place, 4) >= 2, lax.rem(place, 2) == 1
    for up, below, above in ((far, 0, 3), (near, 1, 2), (~far, 0, 3), (~near, 1, 2)):
        yield jnp.where(up, below, above), jnp.where(up, above, below)


def vmem():
    return pl.BlockSpec(memory_space=pltpu.VMEM)


def smem():
    return pl.BlockSpec(memory_space=pltpu.SMEM)


def limit(size):
    return pltpu.CompilerParams(vmem_limit_bytes=size)


def pick_kernel(place_ref, send_ref, tiles_ref, primal_ref, *out_refs):
    total = tiles_ref[0].astype(F32)
    for j in range(1, tiles_ref.shape[0]):
        total = total + tiles_ref[j].astype(F32)
    primal_ref[...] = total.astype(BF16)
    size = out_refs[0].shape[2]
    for (sent, _), out_ref in zip(lists_of_pairings(place_ref[0]), out_refs):
        for t in range(out_ref.shape[0]):
            start = pl.multiple_of(send_ref[sent, t] * size, size)
            out_ref[t] = primal_ref[:, pl.ds(start, size)]


def sum_and_pick(place, lists, tiles, size):
    _, share, unknowns = tiles.shape
    count, length = lists.shape
    return pl.pallas_call(
        pick_kernel,
        out_shape=[jax.ShapeDtypeStruct((share, unknowns), BF16)]
        + [jax.ShapeDtypeStruct((length, share, size), BF16)] * count,
        in_specs=[smem(), smem(), vmem()],
        out_specs=[vmem()] * (1 + count),
        compiler_params=limit(SMALL),
    )(place, lists, tiles)


def apply_kernel(place_ref, counts_ref, cols_ref, primal_ref, *refs):
    *ghost_refs, op_hbm, applied_ref, both_ref, held, op_ref, sems = refs
    rows, slots, size, _ = op_ref.shape
    share = primal_ref.shape[0]
    ways, _, piece = both_ref.shape
    per = piece // size
    part = rows // PARTS
    copies = []
    for i in range(PARTS):
        cut = pl.ds(i * part, part)
        copies.append(pltpu.make_async_copy(op_hbm.at[cut], op_ref.at[cut], sems.at[i]))
        copies[-1].start()
    for b in range(rows):
        held[b] = primal_ref[:, b * size : (b + 1) * size]
    for (_, received), ghost_ref in zip(lists_of_pairings(place_ref[0]), ghost_refs):
        length = ghost_ref.shape[0]
        held[pl.ds(rows + received * length, length)] = ghost_ref[...]
    for w in range(ways):
        both_ref[w, share:, :] = primal_ref[:, w * piece : (w + 1) * piece]
    for r in range(rows):
        if r % part == 0:
            copies[r // part].wait()
        blocks = []
        for k in range(slots):
            block = held[cols_ref[r, k]]
            blocks.append(jnp.where(k < counts_ref[r], block, jnp.zeros_like(block)))
        out = lax.dot_general(
            jnp.concatenate(blocks, axis=1),
            jnp.concatenate([op_ref[r, k] for k in range(slots)], axis=1),
            (((1,), (1,)), ((), ())),
            preferred_element_type=F32,
        ).astype(BF16)
        applied_ref[:, r * size : (r + 1) * size] = out
        both_ref[r // per, :share, (r % per) * size : (r % per + 1) * size] = out


def applied_and_laid_out(place, counts, cols, primal, ghosts, op_blocks, ways):
    share, unknowns = primal.shape
    rows, slots, size, _ = op_blocks.shape
    held = rows + sum(g.shape[0] for g in ghosts)
    return pl.pallas_call(
        apply_kernel,
        out_shape=[
            jax.ShapeDtypeStruct((share, unknowns), BF16),
            jax.ShapeDtypeStruct((ways, 2 * share, unknowns // ways), BF16),
        ],
        in_specs=[smem()] * 3
        + [vmem()] * (1 + len(ghosts))
        + [pl.BlockSpec(memory_space=pltpu.HBM)],
        out_specs=[vmem(), vmem()],
        scratch_shapes=[
            pltpu.VMEM((held, share, size), BF16),
            pltpu.VMEM(op_blocks.shape, BF16),
            pltpu.SemaphoreType.DMA((PARTS,)),
        ],
        compiler_params=limit(LARGE),
    )(place, counts, cols, primal, *ghosts, op_blocks)


def per_device(
    snaps_primal, snaps_adjoint, coef_primal, coef_adjoint, op_blocks, counts, col_index, ghost_send
):
    ways, space = lax.axis_size("snap"), lax.axis_size("space")
    modes = coef_primal.shape[1]
    share = modes // ways
    unknowns = snaps_primal.shape[1]
    piece = unknowns // ways
    size = op_blocks.shape[2]
    deep = space // 2
    along_z = [[h * deep + z * 2 + c for z in range(deep // 2)] for h in range(2) for c in range(2)]
    across_z = [[h * deep + z * 2 + c for h in range(2) for c in range(2)] for z in range(deep // 2)]
    around = [[p * ways + s for s in range(ways) for p in group] for group in across_z]
    place = lax.axis_index("space").reshape(1).astype(jnp.int32)

    primal_part = jnp.einsum("mr,ms->rs", coef_primal, snaps_primal, preferred_element_type=F32)
    primal_tiles = exchange(primal_part.astype(BF16).reshape(ways, share, unknowns), "snap")

    adjoint_part = jnp.einsum("mr,ms->rs", coef_adjoint, snaps_adjoint, preferred_element_type=F32)
    adjoint_tiles = jnp.moveaxis(adjoint_part.astype(BF16).reshape(modes, ways, piece), 1, 0)

    primal, *outgoing = sum_and_pick(place, ghost_send[0], primal_tiles, size)
    adjoint_tiles, _ = lax.optimization_barrier((adjoint_tiles, primal))
    adjoint_tiles = exchange(adjoint_tiles, "snap")
    ghosts = [swapped(o, "space", w) for o, w in zip(outgoing, space_pairings(space))]
    applied, both = applied_and_laid_out(place, counts, col_index, primal, ghosts, op_blocks, ways)

    both = exchange(both, "snap")
    adjoint = adjoint_tiles.astype(F32).sum(axis=0).astype(BF16)
    products = jnp.einsum("was,bs->wab", both, adjoint, preferred_element_type=F32).astype(BF16)
    rows = 2 * share // NEAR
    tiles = exchange(products.reshape(ways * NEAR, rows, modes), ("space", "snap"), around)
    total = tiles.astype(F32).sum(axis=0).astype(BF16)
    every = exchange(jnp.broadcast_to(total[None], (deep // 2, rows, modes)), "space", along_z)
    total = every.astype(F32).sum(axis=0) * (1.0 / math.sqrt(unknowns * space))
    total = exchange(jnp.broadcast_to(total[None], (NEAR, rows, modes)), "space", across_z)
    total = total.reshape(2 * share, modes)
    return (primal, applied, total[:share].T, total[share:].T)


def solution(mesh):
    placed = (
        P("snap", "space"),
        P("snap", "space"),
        P("snap", None),
        P("snap", None),
        P("space", None, None, None),
        P("space"),
        P("space", None),
        P("space", None, None),
    )
    return jax.shard_map(
        per_device,
        mesh=mesh,
        in_specs=placed,
        out_specs=(P("snap", "space"), P("snap", "space"), P(None, "snap"), P(None, "snap")),
        check_vma=False,
    )
```

time: 132 us -> 128 us (0.970)
  waiting for transfers between devices: 26.7 us -> 23.1 us
  starting transfers between devices: 33.5 us -> 32 us
    ppermute x5 -> x4, waiting for transfers between devices: 8.19 us -> 0.18 us  [swapped(): lax.ppermute(value, axis, [(a, b) for a, b in pairs] + [(b, a) for a, b i...]
    all_to_all x3, waiting for transfers between devices: 18.5 us -> 22.9 us  [exchange(): lax.all_to_all(tiles, axis, 0, 0, tiled=True, axis_index_groups=groups)]
    ppermute x5 -> x4, starting transfers between devices: 19.3 us -> 16.1 us  [swapped(): lax.ppermute(value, axis, [(a, b) for a, b in pairs] + [(b, a) for a, b i...]
    all_to_all x3, starting transfers between devices: 14.2 us -> 15.9 us  [exchange(): lax.all_to_all(tiles, axis, 0, 0, tiled=True, axis_index_groups=groups)]
    unnamed x19 -> x17, local copies, waits for them, and re-layouts: 3.63 us -> 3.34 us
  transfers between devices with their start and end apart: 8 -> 7, of which waited for: 5 -> 3; matrix products, arithmetic and copies ran while one was open for 3% -> 4% of each run, Pallas kernels for 4% -> 4%
where the time goes in v4:
time: 128 us; the launch traced here: 127 us
  blocking collectives  52.3 us (41%)
  starting transfers between devices  32 us (25%)
  waiting for transfers between devices  23.1 us (18%)
  Pallas kernels  6.58 us (5%)
  matrix products  5.9 us (5%)
  local copies, waits for them, and re-layouts  5.33 us (4%)
    all_to_all x3, blocking collectives, exchange(): lax.all_to_all(tiles, axis, 0, 0, tiled=True, axis_index_groups=groups)  52.3 us
    all_to_all x3, waiting for transfers between devices, exchange(): lax.all_to_all(tiles, axis, 0, 0, tiled=True, axis_index_groups=groups)  22.9 us
    ppermute x4, starting transfers between devices, swapped(): lax.ppermute(value, axis, [(a, b) for a, b in pairs] + [(b, a) for a, b i...  16.1 us
    all_to_all x3, starting transfers between devices, exchange(): lax.all_to_all(tiles, axis, 0, 0, tiled=True, axis_index_groups=groups)  15.9 us
    pallas_call x1, Pallas kernels, applied_and_laid_out(): pl.pallas_call(apply_kernel, out_shape=[jax.ShapeDtypeStruct((share, unkn...  5.02 us
    unnamed x17, local copies, waits for them, and re-layouts  3.34 us
    dot_general x1, matrix products, per_device(): jnp.einsum('mr,ms->rs', coef_primal, snaps_primal, preferred_element_type...  2.65 us
  transfers between devices with their start and end apart: 7, of which 3 were waited for; matrix products, arithmetic and copies ran while one was open for 4% of the time, Pallas kernels for 4%

profile of v4, /device:TPU:1, one launch (start us, length us, event | category | flops | bytes accessed | tf_op | source)
XLA Modules:
  0.0 126.9 jit_solution(1189889567608134738)
XLA Ops:
  0.6 1.4 %copy-done = bf16[256,3072]{1,0:T(8,128)(2,1)S(1)} copy-done((bf16[256,3072]{1,0:T(8,128)(2,1)S(1)}, bf16[256,3072]{1,0:T(8,128)(2,1)}, u32[]{:S(2)}) %copy-start) | copy-done | bytes 1572888
  2.0 2.7 %convolution_convert_fusion.1 = bf16[256,3072]{1,0:T(8,128)(2,1)} fusion(bf16[256,256]{1,0:T(8,128)(2,1)} %param.10, bf16[256,3072]{1,0:T(8,128)(2,1)S(1)} %copy-done), kind=kOutput, calls=%fused_computation.1 | convolution fusion | flops 403439616 | bytes 3276800 | tf_op jit(solution)/shard_map/mr,ms->rs/dot_general | solution.py:150
  4.7 6.0 %all-to-all-start = ((bf16[8,32,3072]{2,1,0:T(8,128)(2,1)}), bf16[8,32,3072]{2,1,0:T(8,128)(2,1)S(1)}, u32[]{:S(2)}, u32[]{:S(2)}) async-start(bf16[8,32,3072]{2,1,0:T(8,128)(2,1)} %bitcast.27), calls=%async_computation | async-start | bytes 3145728 | tf_op jit(solution)/shard_map/all_to_all | solution.py:18
  10.7 2.0 %convolution_convert_fusion = bf16[256,3072]{1,0:T(8,128)(2,1)S(1)} fusion(bf16[256,256]{1,0:T(8,128)(2,1)S(1)} %copy-done.2, bf16[256,3072]{1,0:T(8,128)(2,1)} %param.9), kind=kOutput, calls=%fused_computation | convolution fusion | flops 403439616 | bytes 3276800 | tf_op jit(solution)/shard_map/mr,ms->rs/dot_general | solution.py:153
  12.7 1.3 %copy.19 = bf16[32,8,8,384]{3,2,0,1:T(8,128)(2,1)} copy(bf16[32,8,8,384]{3,2,1,0:T(8,128)(2,1)S(1)} %bitcast.28) | data formatting | bytes 3145728 | tf_op jit(solution)/shard_map/reshape | solution.py:154
  14.1 15.8 %all-to-all-done.tiles_ref = bf16[8,32,3072]{2,1,0:T(8,128)(2,1)S(1)} async-done(((bf16[8,32,3072]{2,1,0:T(8,128)(2,1)}), bf16[8,32,3072]{2,1,0:T(8,128)(2,1)S(1)}, u32[]{:S(2)}, u32[]{:S(2)}) %all-to-all-start) | async-done | bytes 1572896 | tf_op jit(solution)/shard_map/all_to_all | solution.py:18
  29.9 1.6 %shard_map.111 = (bf16[32,3072]{1,0:T(8,128)(2,1)}, bf16[6,32,128]{2,1,0:T(8,128)(2,1)S(1)}, bf16[6,32,128]{2,1,0:T(8,128)(2,1)S(1)}, bf16[6,32,128]{2,1,0:T(8,128)(2,1)S(1)}, bf16[6,32,128]{2,1,0:T(8,128)(2,1)S(1)}) custom-call(s32[1]{0:T(128)} %bitcast.place_ref, s32[4,6]{1,0:T(4,128)S(1)} %bitcast.25, bf16[8,32,3072]{2,1,0:T(8,128)(2,1)S(1)} %all-to-all-done.tiles_ref), custom_call_target="tpu_custom_call" | custom-call | tf_op jit(solution)/shard_map/pallas_call | solution.py:66
  31.5 4.6 %all-to-all-start.2 = ((bf16[8,256,384]{2,1,0:T(8,128)(2,1)}), bf16[8,256,384]{2,1,0:T(8,128)(2,1)S(1)}, u32[]{:S(2)}, u32[]{:S(2)}) async-start(bf16[8,256,384]{2,1,0:T(8,128)(2,1)} %bitcast.26), calls=%async_computation.2 | async-start | bytes 3145728 | tf_op jit(solution)/shard_map/all_to_all | solution.py:18
  36.0 0.7 collective-permute-start
  36.7 11.2 %collective-permute-start.1 = (bf16[6,32,128]{2,1,0:T(8,128)(2,1)S(1)}, bf16[6,32,128]{2,1,0:T(8,128)(2,1)S(1)}, u32[]{:S(2)}, u32[]{:S(2)}) collective-permute-start(bf16[6,32,128]{2,1,0:T(8,128)(2,1)S(1)} %get-tuple-element.14), channel_id=1, source_target_pairs={{8,16},{24,32},{40,48},{56,64},{72,80},{88,96},{104,112},{120,128}... | collective-permute-start | bytes 147464 | tf_op jit(solution)/shard_map/ppermute | solution.py:22
  47.9 1.9 %collective-permute-start.2 = (bf16[6,32,128]{2,1,0:T(8,128)(2,1)S(1)}, bf16[6,32,128]{2,1,0:T(8,128)(2,1)S(1)}, u32[]{:S(2)}, u32[]{:S(2)}) collective-permute-start(bf16[6,32,128]{2,1,0:T(8,128)(2,1)S(1)} %get-tuple-element.15), channel_id=1, source_target_pairs={{0,16},{8,24},{32,48},{40,56},{64,80},{72,88},{96,112},{104,120},{... | collective-permute-start | bytes 147464 | tf_op jit(solution)/shard_map/ppermute | solution.py:22
  49.8 2.3 %collective-permute-start.3 = (bf16[6,32,128]{2,1,0:T(8,128)(2,1)S(1)}, bf16[6,32,128]{2,1,0:T(8,128)(2,1)S(1)}, u32[]{:S(2)}, u32[]{:S(2)}) collective-permute-start(bf16[6,32,128]{2,1,0:T(8,128)(2,1)S(1)} %get-tuple-element.16), channel_id=1, source_target_pairs={{0,8},{16,24},{32,40},{48,56},{64,72},{80,88},{96,104},{112,120},{... | collective-permute-start | bytes 147464 | tf_op jit(solution)/shard_map/ppermute | solution.py:22
  52.2 0.7 copy.15.cols_ref
  53.1 0.4 copy-done.3
  53.7 0.6 copy-done.6
  54.3 5.0 %shard_map.112 = (bf16[32,3072]{1,0:T(8,128)(2,1)}, bf16[8,64,384]{2,1,0:T(8,128)(2,1)}) custom-call(s32[1]{0:T(128)} %bitcast.place_ref, s32[24]{0:T(128)} %counts_ref.1, s32[24,5]{1,0:T(8,128)} %copy.15.cols_ref, bf16[32,3072]{1,0:T(8,128)(2,1)} %get-tuple-element.8.primal_ref, bf16[6,32,128]{2,1,0:T(8,128)(2,1)} %copy-done.3, ...), custom_call_target="tpu_custom_call" | custom-call | tf_op jit(solution)/shard_map/pallas_call | solution.py:116
  59.3 5.3 %all-to-all-start.1 = ((bf16[8,64,384]{2,1,0:T(8,128)(2,1)}), bf16[8,64,384]{2,1,0:T(8,128)(2,1)S(1)}, u32[]{:S(2)}, u32[]{:S(2)}) async-start(bf16[8,64,384]{2,1,0:T(8,128)(2,1)} %get-tuple-element.18), calls=%async_computation.1 | async-start | bytes 786432 | tf_op jit(solution)/shard_map/all_to_all | solution.py:18
  64.7 0.9 reduce_sum.33
  65.6 7.0 %all-to-all-done.1 = bf16[8,64,384]{2,1,0:T(8,128)(2,1)S(1)} async-done(((bf16[8,64,384]{2,1,0:T(8,128)(2,1)}), bf16[8,64,384]{2,1,0:T(8,128)(2,1)S(1)}, u32[]{:S(2)}, u32[]{:S(2)}) %all-to-all-start.1) | async-done | bytes 393248 | tf_op jit(solution)/shard_map/all_to_all | solution.py:18
  72.6 1.2 convolution_convert_fusion.2
  73.9 22.3 %all_to_all.30 = bf16[32,16,256]{2,1,0:T(8,128)(2,1)S(1)} all-to-all(bf16[32,16,256]{2,1,0:T(8,128)(2,1)S(1)} %bitcast.29), channel_id=1, replica_groups={{0,8,256,264,1,9,257,265,2,10,258,266,3,11,259,267,4,12,260,268,5,13,26..., dimensions={0} | all-to-all | bytes 524288 | tf_op jit(solution)/shard_map/all_to_all | solution.py:18
  96.2 19.5 %all_to_all.31 = bf16[16,16,256]{2,1,0:T(8,128)(2,1)S(1)} all-to-all(bf16[16,16,256]{2,1,0:T(8,128)(2,1)S(1)} %broadcast_in_dim.4), channel_id=1, replica_groups={{0,16,32,48,64,80,96,112,128,144,160,176,192,208,224,240},{8,24,40,56,7..., dimensions={0} | all-to-all | bytes 262144 | tf_op jit(solution)/shard_map/all_to_all | solution.py:18
  115.8 10.5 %all_to_all.32 = f32[4,16,256]{2,1,0:T(8,128)S(1)} all-to-all(f32[4,16,256]{2,1,0:T(8,128)S(1)} %broadcast_in_dim.5), channel_id=1, replica_groups={{0,8,256,264},{16,24,272,280},{32,40,288,296},{48,56,304,312},{64,72,32..., dimensions={0} | all-to-all | bytes 131072 | tf_op jit(solution)/shard_map/all_to_all | solution.py:18
  126.3 0.6 fusion.1
  (23 shorter events, 0.5 us)
Async XLA Ops:
  0.6 1.4 %copy-start = (bf16[256,3072]{1,0:T(8,128)(2,1)S(1)}, bf16[256,3072]{1,0:T(8,128)(2,1)}, u32[]{:S(2)}) copy-start(bf16[256,3072]{1,0:T(8,128)(2,1)} %param.8) | copy-start | bytes 4718596
  4.7 6.0 %copy-start.2 = (bf16[256,256]{1,0:T(8,128)(2,1)S(1)}, bf16[256,256]{1,0:T(8,128)(2,1)}, u32[]{:S(2)}) copy-start(bf16[256,256]{1,0:T(8,128)(2,1)} %param.11) | copy-start | bytes 393220
  4.7 25.2 %all-to-all-start = ((bf16[8,32,3072]{2,1,0:T(8,128)(2,1)}), bf16[8,32,3072]{2,1,0:T(8,128)(2,1)S(1)}, u32[]{:S(2)}, u32[]{:S(2)}) async-start(bf16[8,32,3072]{2,1,0:T(8,128)(2,1)} %bitcast.27), calls=%async_computation | async-start | bytes 3145728 | tf_op jit(solution)/shard_map/all_to_all | solution.py:18
  12.7 17.2 %copy-start.1 = (s32[1,4,6]{2,1,0:T(4,128)S(1)}, s32[1,4,6]{2,1,0:T(4,128)}, u32[]{:S(2)}) copy-start(s32[1,4,6]{2,1,0:T(4,128)} %param.15) | copy-start | bytes 292
  31.4 20.7 %copy-start.7 = (s32[24,5]{0,1:T(8,128)S(1)}, s32[24,5]{0,1:T(8,128)}, u32[]{:S(2)}) copy-start(s32[24,5]{0,1:T(8,128)} %param.14) | copy-start | bytes 1444
  31.5 27.9 %all-to-all-start.2 = ((bf16[8,256,384]{2,1,0:T(8,128)(2,1)}), bf16[8,256,384]{2,1,0:T(8,128)(2,1)S(1)}, u32[]{:S(2)}, u32[]{:S(2)}) async-start(bf16[8,256,384]{2,1,0:T(8,128)(2,1)} %bitcast.26), calls=%async_computation.2 | async-start | bytes 3145728 | tf_op jit(solution)/shard_map/all_to_all | solution.py:18
  36.0 16.8 %collective-permute-start = (bf16[6,32,128]{2,1,0:T(8,128)(2,1)S(1)}, bf16[6,32,128]{2,1,0:T(8,128)(2,1)S(1)}, u32[]{:S(2)}, u32[]{:S(2)}) collective-permute-start(bf16[6,32,128]{2,1,0:T(8,128)(2,1)S(1)} %get-tuple-element.13), channel_id=1, source_target_pairs={{16,32},{24,40},{48,64},{56,72},{80,96},{88,104},{112,128},{120,13... | collective-permute-start | bytes 147464 | tf_op jit(solution)/shard_map/ppermute | solution.py:22
  36.7 16.2 %collective-permute-start.1 = (bf16[6,32,128]{2,1,0:T(8,128)(2,1)S(1)}, bf16[6,32,128]{2,1,0:T(8,128)(2,1)S(1)}, u32[]{:S(2)}, u32[]{:S(2)}) collective-permute-start(bf16[6,32,128]{2,1,0:T(8,128)(2,1)S(1)} %get-tuple-element.14), channel_id=1, source_target_pairs={{8,16},{24,32},{40,48},{56,64},{72,80},{88,96},{104,112},{120,128}... | collective-permute-start | bytes 147464 | tf_op jit(solution)/shard_map/ppermute | solution.py:22
  47.9 5.1 %collective-permute-start.2 = (bf16[6,32,128]{2,1,0:T(8,128)(2,1)S(1)}, bf16[6,32,128]{2,1,0:T(8,128)(2,1)S(1)}, u32[]{:S(2)}, u32[]{:S(2)}) collective-permute-start(bf16[6,32,128]{2,1,0:T(8,128)(2,1)S(1)} %get-tuple-element.15), channel_id=1, source_target_pairs={{0,16},{8,24},{32,48},{40,56},{64,80},{72,88},{96,112},{104,120},{... | collective-permute-start | bytes 147464 | tf_op jit(solution)/shard_map/ppermute | solution.py:22
  49.8 3.2 %collective-permute-start.3 = (bf16[6,32,128]{2,1,0:T(8,128)(2,1)S(1)}, bf16[6,32,128]{2,1,0:T(8,128)(2,1)S(1)}, u32[]{:S(2)}, u32[]{:S(2)}) collective-permute-start(bf16[6,32,128]{2,1,0:T(8,128)(2,1)S(1)} %get-tuple-element.16), channel_id=1, source_target_pairs={{0,8},{16,24},{32,40},{48,56},{64,72},{80,88},{96,104},{112,120},{... | collective-permute-start | bytes 147464 | tf_op jit(solution)/shard_map/ppermute | solution.py:22
  52.9 0.6 copy-start.3
  52.9 0.6 copy-start.4
  53.0 0.6 copy-start.5
  53.7 0.6 copy-start.6
  59.3 13.3 %all-to-all-start.1 = ((bf16[8,64,384]{2,1,0:T(8,128)(2,1)}), bf16[8,64,384]{2,1,0:T(8,128)(2,1)S(1)}, u32[]{:S(2)}, u32[]{:S(2)}) async-start(bf16[8,64,384]{2,1,0:T(8,128)(2,1)} %get-tuple-element.18), calls=%async_computation.1 | async-start | bytes 786432 | tf_op jit(solution)/shard_map/all_to_all | solution.py:18

commit v5 on v4

--- a/solution.py
+++ b/solution.py
@@ -97,7 +97,7 @@
             copies[r // part].wait()
         blocks = []
         for k in range(slots):
-            block = held[cols_ref[r, k]]
+            block = held[cols_ref[k, r]]
             blocks.append(jnp.where(k < counts_ref[r], block, jnp.zeros_like(block)))
         out = lax.dot_general(
             jnp.concatenate(blocks, axis=1),
@@ -144,22 +144,25 @@
     deep = space // 2
     along_z = [[h * deep + z * 2 + c for z in range(deep // 2)] for h in range(2) for c in range(2)]
     across_z = [[h * deep + z * 2 + c for h in range(2) for c in range(2)] for z in range(deep // 2)]
-    around = [[p * ways + s for s in range(ways) for p in group] for group in across_z]
+    turns = [0, 3, 4, 7, 2, 1, 6, 5]
+    around = [[p * ways + s for s in turns for p in group] for group in across_z]
     place = lax.axis_index("space").reshape(1).astype(jnp.int32)
 
-    primal_part = jnp.einsum("mr,ms->rs", coef_primal, snaps_primal, preferred_element_type=F32)
-    primal_tiles = exchange(primal_part.astype(BF16).reshape(ways, share, unknowns), "snap")
+    coef_turned = jnp.concatenate([coef_primal[:, s * share : (s + 1) * share] for s in turns], axis=1)
+    primal_part = jnp.einsum("mr,ms->rs", coef_turned, snaps_primal, preferred_element_type=F32)
+    primal_tiles = primal_part.astype(BF16).reshape(ways, share, unknowns)
+    primal_tiles = exchange(primal_tiles, "snap", [turns])
 
     adjoint_part = jnp.einsum("mr,ms->rs", coef_adjoint, snaps_adjoint, preferred_element_type=F32)
     adjoint_tiles = jnp.moveaxis(adjoint_part.astype(BF16).reshape(modes, ways, piece), 1, 0)
 
     primal, *outgoing = sum_and_pick(place, ghost_send[0], primal_tiles, size)
     adjoint_tiles, _ = lax.optimization_barrier((adjoint_tiles, primal))
-    adjoint_tiles = exchange(adjoint_tiles, "snap")
+    adjoint_tiles = exchange(adjoint_tiles, "snap", [turns])
     ghosts = [swapped(o, "space", w) for o, w in zip(outgoing, space_pairings(space))]
-    applied, both = applied_and_laid_out(place, counts, col_index, primal, ghosts, op_blocks, ways)
+    applied, both = applied_and_laid_out(place, counts, col_index.T, primal, ghosts, op_blocks, ways)
 
-    both = exchange(both, "snap")
+    both = exchange(both, "snap", [turns])
     adjoint = adjoint_tiles.astype(F32).sum(axis=0).astype(BF16)
     products = jnp.einsum("was,bs->wab", both, adjoint, preferred_element_type=F32).astype(BF16)
     rows = 2 * share // NEAR

time: 128 us -> 124 us (0.969)
  starting transfers between devices: 32 us -> 25.8 us
  waiting for transfers between devices: 23.1 us -> 27.5 us
    all_to_all x3, waiting for transfers between devices: 22.9 us -> 26.6 us  [exchange(): lax.all_to_all(tiles, axis, 0, 0, tiled=True, axis_index_groups=groups)]
    ppermute x4, starting transfers between devices: 16.1 us -> 12.7 us  [swapped(): lax.ppermute(value, axis, [(a, b) for a, b in pairs] + [(b, a) for a, b i...]
    all_to_all x3, starting transfers between devices: 15.9 us -> 13 us  [exchange(): lax.all_to_all(tiles, axis, 0, 0, tiled=True, axis_index_groups=groups)]
    unnamed x17 -> x14, local copies, waits for them, and re-layouts: 3.34 us -> 0.64 us
    slice x0 -> x2, local copies, waits for them, and re-layouts: none -> 2.27 us  [per_device(): coef_primal[:, s * share:(s + 1) * share]]
  transfers between devices with their start and end apart: 7 -> 7, of which waited for: 3 -> 4; matrix products, arithmetic and copies ran while one was open for 4% -> 3% of each run, Pallas kernels for 4% -> 4%
where the time goes in v5:
time: 124 us; the launch traced here: 123 us
  blocking collectives  51.3 us (41%)
  waiting for transfers between devices  27.5 us (22%)
  starting transfers between devices  25.8 us (21%)
  Pallas kernels  6.58 us (5%)
  local copies, waits for them, and re-layouts  5.1 us (4%)
  matrix products  5 us (4%)
    all_to_all x3, blocking collectives, exchange(): lax.all_to_all(tiles, axis, 0, 0, tiled=True, axis_index_groups=groups)  51.3 us
    all_to_all x3, waiting for transfers between devices, exchange(): lax.all_to_all(tiles, axis, 0, 0, tiled=True, axis_index_groups=groups)  26.6 us
    all_to_all x3, starting transfers between devices, exchange(): lax.all_to_all(tiles, axis, 0, 0, tiled=True, axis_index_groups=groups)  13 us
    ppermute x4, starting transfers between devices, swapped(): lax.ppermute(value, axis, [(a, b) for a, b in pairs] + [(b, a) for a, b i...  12.7 us
    pallas_call x1, Pallas kernels, applied_and_laid_out(): pl.pallas_call(apply_kernel, out_shape=[jax.ShapeDtypeStruct((share, unkn...  5.02 us
  transfers between devices with their start and end apart: 7, of which 4 were waited for; matrix products, arithmetic and copies ran while one was open for 3% of the time, Pallas kernels for 4%

profile of v5, /device:TPU:1, one launch (start us, length us, event | category | flops | bytes accessed | tf_op | source)
XLA Modules:
  0.0 123.0 jit_solution(12215992181954032284)
XLA Ops:
  0.6 1.1 slice.36
  1.8 1.2 fusion.1
  3.1 1.7 %convolution_convert_fusion.1 = bf16[256,3072]{1,0:T(8,128)(2,1)} fusion(bf16[256,256]{1,0:T(8,128)(2,1)S(1)} %concatenate.4, bf16[256,3072]{1,0:T(8,128)(2,1)S(1)} %copy-done), kind=kOutput, calls=%fused_computation.1 | convolution fusion | flops 403439616 | bytes 3276800 | tf_op jit(solution)/shard_map/mr,ms->rs/dot_general | solution.py:152
  4.9 6.0 %all-to-all-start = ((bf16[8,32,3072]{2,1,0:T(8,128)(2,1)}), bf16[8,32,3072]{2,1,0:T(8,128)(2,1)S(1)}, u32[]{:S(2)}, u32[]{:S(2)}) async-start(bf16[8,32,3072]{2,1,0:T(8,128)(2,1)} %bitcast.28), calls=%async_computation | async-start | bytes 3145728 | tf_op jit(solution)/shard_map/all_to_all | solution.py:18
  10.9 2.0 %convolution_convert_fusion = bf16[256,3072]{1,0:T(8,128)(2,1)S(1)} fusion(bf16[256,256]{1,0:T(8,128)(2,1)S(1)} %copy-done.2, bf16[256,3072]{1,0:T(8,128)(2,1)} %param.9), kind=kOutput, calls=%fused_computation | convolution fusion | flops 403439616 | bytes 3276800 | tf_op jit(solution)/shard_map/mr,ms->rs/dot_general | solution.py:156
  12.9 1.3 %copy.16 = bf16[32,8,8,384]{3,2,0,1:T(8,128)(2,1)} copy(bf16[32,8,8,384]{3,2,1,0:T(8,128)(2,1)S(1)} %bitcast.29) | data formatting | bytes 3145728 | tf_op jit(solution)/shard_map/reshape | solution.py:157
  14.2 17.6 %all-to-all-done.tiles_ref = bf16[8,32,3072]{2,1,0:T(8,128)(2,1)S(1)} async-done(((bf16[8,32,3072]{2,1,0:T(8,128)(2,1)}), bf16[8,32,3072]{2,1,0:T(8,128)(2,1)S(1)}, u32[]{:S(2)}, u32[]{:S(2)}) %all-to-all-start) | async-done | bytes 1572896 | tf_op jit(solution)/shard_map/all_to_all | solution.py:18
  31.9 1.6 %shard_map.111 = (bf16[32,3072]{1,0:T(8,128)(2,1)}, bf16[6,32,128]{2,1,0:T(8,128)(2,1)S(1)}, bf16[6,32,128]{2,1,0:T(8,128)(2,1)S(1)}, bf16[6,32,128]{2,1,0:T(8,128)(2,1)S(1)}, bf16[6,32,128]{2,1,0:T(8,128)(2,1)S(1)}) custom-call(s32[1]{0:T(128)} %bitcast.place_ref, s32[4,6]{1,0:T(4,128)S(1)} %bitcast.26, bf16[8,32,3072]{2,1,0:T(8,128)(2,1)S(1)} %all-to-all-done.tiles_ref), custom_call_target="tpu_custom_call" | custom-call | tf_op jit(solution)/shard_map/pallas_call | solution.py:66
  33.5 3.6 %all-to-all-start.2 = ((bf16[8,256,384]{2,1,0:T(8,128)(2,1)}), bf16[8,256,384]{2,1,0:T(8,128)(2,1)S(1)}, u32[]{:S(2)}, u32[]{:S(2)}) async-start(bf16[8,256,384]{2,1,0:T(8,128)(2,1)} %bitcast.27), calls=%async_computation.2 | async-start | bytes 3145728 | tf_op jit(solution)/shard_map/all_to_all | solution.py:18
  37.0 0.7 collective-permute-start
  37.7 7.8 %collective-permute-start.1 = (bf16[6,32,128]{2,1,0:T(8,128)(2,1)S(1)}, bf16[6,32,128]{2,1,0:T(8,128)(2,1)S(1)}, u32[]{:S(2)}, u32[]{:S(2)}) collective-permute-start(bf16[6,32,128]{2,1,0:T(8,128)(2,1)S(1)} %get-tuple-element.14), channel_id=1, source_target_pairs={{8,16},{24,32},{40,48},{56,64},{72,80},{88,96},{104,112},{120,128}... | collective-permute-start | bytes 147464 | tf_op jit(solution)/shard_map/ppermute | solution.py:22
  45.6 1.9 %collective-permute-start.2 = (bf16[6,32,128]{2,1,0:T(8,128)(2,1)S(1)}, bf16[6,32,128]{2,1,0:T(8,128)(2,1)S(1)}, u32[]{:S(2)}, u32[]{:S(2)}) collective-permute-start(bf16[6,32,128]{2,1,0:T(8,128)(2,1)S(1)} %get-tuple-element.15), channel_id=1, source_target_pairs={{0,16},{8,24},{32,48},{40,56},{64,80},{72,88},{96,112},{104,120},{... | collective-permute-start | bytes 147464 | tf_op jit(solution)/shard_map/ppermute | solution.py:22
  47.5 2.3 %collective-permute-start.3 = (bf16[6,32,128]{2,1,0:T(8,128)(2,1)S(1)}, bf16[6,32,128]{2,1,0:T(8,128)(2,1)S(1)}, u32[]{:S(2)}, u32[]{:S(2)}) collective-permute-start(bf16[6,32,128]{2,1,0:T(8,128)(2,1)S(1)} %get-tuple-element.16), channel_id=1, source_target_pairs={{0,8},{16,24},{32,40},{48,56},{64,72},{80,88},{96,104},{112,120},{... | collective-permute-start | bytes 147464 | tf_op jit(solution)/shard_map/ppermute | solution.py:22
  49.9 0.8 collective-permute-done.2.refs_2_
  51.3 5.0 %shard_map.112 = (bf16[32,3072]{1,0:T(8,128)(2,1)}, bf16[8,64,384]{2,1,0:T(8,128)(2,1)}) custom-call(s32[1]{0:T(128)} %bitcast.place_ref, s32[24]{0:T(128)} %counts_ref.1, s32[5,24]{1,0:T(8,128)} %bitcast.33, bf16[32,3072]{1,0:T(8,128)(2,1)} %get-tuple-element.8.primal_ref, bf16[6,32,128]{2,1,0:T(8,128)(2,1)} %copy-done.3, bf16[6,32,128]{2,1,0:T(8,128)(2,1)} %copy-done.4, ...), custom_call_target="tpu_custom_call" | custom-call | tf_op jit(solution)/shard_map/pallas_call | solution.py:116
  56.4 2.0 %all-to-all-done.2 = bf16[8,256,384]{2,1,0:T(8,128)(2,1)S(1)} async-done(((bf16[8,256,384]{2,1,0:T(8,128)(2,1)}), bf16[8,256,384]{2,1,0:T(8,128)(2,1)S(1)}, u32[]{:S(2)}, u32[]{:S(2)}) %all-to-all-start.2) | async-done | bytes 1572896 | tf_op jit(solution)/shard_map/all_to_all | solution.py:18
  58.4 3.5 %all-to-all-start.1 = ((bf16[8,64,384]{2,1,0:T(8,128)(2,1)}), bf16[8,64,384]{2,1,0:T(8,128)(2,1)S(1)}, u32[]{:S(2)}, u32[]{:S(2)}) async-start(bf16[8,64,384]{2,1,0:T(8,128)(2,1)} %get-tuple-element.18), calls=%async_computation.1 | async-start | bytes 786432 | tf_op jit(solution)/shard_map/all_to_all | solution.py:18
  61.9 0.9 reduce_sum.33
  62.8 6.9 %all-to-all-done.1 = bf16[8,64,384]{2,1,0:T(8,128)(2,1)S(1)} async-done(((bf16[8,64,384]{2,1,0:T(8,128)(2,1)}), bf16[8,64,384]{2,1,0:T(8,128)(2,1)S(1)}, u32[]{:S(2)}, u32[]{:S(2)}) %all-to-all-start.1) | async-done | bytes 393248 | tf_op jit(solution)/shard_map/all_to_all | solution.py:18
  69.7 1.2 %convolution_convert_fusion.2 = bf16[8,64,256]{2,1,0:T(8,128)(2,1)S(1)} fusion(bf16[8,64,384]{2,1,0:T(8,128)(2,1)S(1)} %all-to-all-done.1, bf16[256,384]{1,0:T(8,128)(2,1)} %reduce_sum.33), kind=kOutput, calls=%fused_computation.3 | convolution fusion | flops 100794368 | bytes 851968 | tf_op jit(solution)/shard_map/was,bs->wab/dot_general | solution.py:167
  71.0 22.4 %all_to_all.30 = bf16[32,16,256]{2,1,0:T(8,128)(2,1)S(1)} all-to-all(bf16[32,16,256]{2,1,0:T(8,128)(2,1)S(1)} %bitcast.30), channel_id=1, replica_groups={{0,8,256,264,3,11,259,267,4,12,260,268,7,15,263,271,2,10,258,266,1,9,25..., dimensions={0} | all-to-all | bytes 524288 | tf_op jit(solution)/shard_map/all_to_all | solution.py:18
  93.4 18.7 %all_to_all.31 = bf16[16,16,256]{2,1,0:T(8,128)(2,1)S(1)} all-to-all(bf16[16,16,256]{2,1,0:T(8,128)(2,1)S(1)} %broadcast_in_dim.4), channel_id=1, replica_groups={{0,16,32,48,64,80,96,112,128,144,160,176,192,208,224,240},{8,24,40,56,7..., dimensions={0} | all-to-all | bytes 262144 | tf_op jit(solution)/shard_map/all_to_all | solution.py:18
  112.1 10.3 %all_to_all.32 = f32[4,16,256]{2,1,0:T(8,128)S(1)} all-to-all(f32[4,16,256]{2,1,0:T(8,128)S(1)} %broadcast_in_dim.5), channel_id=1, replica_groups={{0,8,256,264},{16,24,272,280},{32,40,288,296},{48,56,304,312},{64,72,32..., dimensions={0} | all-to-all | bytes 131072 | tf_op jit(solution)/shard_map/all_to_all | solution.py:18
  122.4 0.6 fusion.2
  (23 shorter events, 0.9 us)
Async XLA Ops:
  0.6 2.5 %copy-start = (bf16[256,3072]{1,0:T(8,128)(2,1)S(1)}, bf16[256,3072]{1,0:T(8,128)(2,1)}, u32[]{:S(2)}) copy-start(bf16[256,3072]{1,0:T(8,128)(2,1)} %param.8) | copy-start | bytes 4718596
  4.9 6.0 %copy-start.2 = (bf16[256,256]{1,0:T(8,128)(2,1)S(1)}, bf16[256,256]{1,0:T(8,128)(2,1)}, u32[]{:S(2)}) copy-start(bf16[256,256]{1,0:T(8,128)(2,1)} %param.11) | copy-start | bytes 393220
  4.9 27.0 %all-to-all-start = ((bf16[8,32,3072]{2,1,0:T(8,128)(2,1)}), bf16[8,32,3072]{2,1,0:T(8,128)(2,1)S(1)}, u32[]{:S(2)}, u32[]{:S(2)}) async-start(bf16[8,32,3072]{2,1,0:T(8,128)(2,1)} %bitcast.28), calls=%async_computation | async-start | bytes 3145728 | tf_op jit(solution)/shard_map/all_to_all | solution.py:18
  12.9 19.0 %copy-start.1 = (s32[1,4,6]{2,1,0:T(4,128)S(1)}, s32[1,4,6]{2,1,0:T(4,128)}, u32[]{:S(2)}) copy-start(s32[1,4,6]{2,1,0:T(4,128)} %param.15) | copy-start | bytes 292
  33.5 24.9 %all-to-all-start.2 = ((bf16[8,256,384]{2,1,0:T(8,128)(2,1)}), bf16[8,256,384]{2,1,0:T(8,128)(2,1)S(1)}, u32[]{:S(2)}, u32[]{:S(2)}) async-start(bf16[8,256,384]{2,1,0:T(8,128)(2,1)} %bitcast.27), calls=%async_computation.2 | async-start | bytes 3145728 | tf_op jit(solution)/shard_map/all_to_all | solution.py:18
  37.0 12.8 %collective-permute-start = (bf16[6,32,128]{2,1,0:T(8,128)(2,1)S(1)}, bf16[6,32,128]{2,1,0:T(8,128)(2,1)S(1)}, u32[]{:S(2)}, u32[]{:S(2)}) collective-permute-start(bf16[6,32,128]{2,1,0:T(8,128)(2,1)S(1)} %get-tuple-element.13), channel_id=1, source_target_pairs={{16,32},{24,40},{48,64},{56,72},{80,96},{88,104},{112,128},{120,13... | collective-permute-start | bytes 147464 | tf_op jit(solution)/shard_map/ppermute | solution.py:22
  37.7 12.1 %collective-permute-start.1 = (bf16[6,32,128]{2,1,0:T(8,128)(2,1)S(1)}, bf16[6,32,128]{2,1,0:T(8,128)(2,1)S(1)}, u32[]{:S(2)}, u32[]{:S(2)}) collective-permute-start(bf16[6,32,128]{2,1,0:T(8,128)(2,1)S(1)} %get-tuple-element.14), channel_id=1, source_target_pairs={{8,16},{24,32},{40,48},{56,64},{72,80},{88,96},{104,112},{120,128}... | collective-permute-start | bytes 147464 | tf_op jit(solution)/shard_map/ppermute | solution.py:22
  45.6 5.1 %collective-permute-start.2 = (bf16[6,32,128]{2,1,0:T(8,128)(2,1)S(1)}, bf16[6,32,128]{2,1,0:T(8,128)(2,1)S(1)}, u32[]{:S(2)}, u32[]{:S(2)}) collective-permute-start(bf16[6,32,128]{2,1,0:T(8,128)(2,1)S(1)} %get-tuple-element.15), channel_id=1, source_target_pairs={{0,16},{8,24},{32,48},{40,56},{64,80},{72,88},{96,112},{104,120},{... | collective-permute-start | bytes 147464 | tf_op jit(solution)/shard_map/ppermute | solution.py:22
  47.5 3.2 %collective-permute-start.3 = (bf16[6,32,128]{2,1,0:T(8,128)(2,1)S(1)}, bf16[6,32,128]{2,1,0:T(8,128)(2,1)S(1)}, u32[]{:S(2)}, u32[]{:S(2)}) collective-permute-start(bf16[6,32,128]{2,1,0:T(8,128)(2,1)S(1)} %get-tuple-element.16), channel_id=1, source_target_pairs={{0,8},{16,24},{32,40},{48,56},{64,72},{80,88},{96,104},{112,120},{... | collective-permute-start | bytes 147464 | tf_op jit(solution)/shard_map/ppermute | solution.py:22
  49.8 0.9 copy-start.3
  49.8 0.9 copy-start.4
  50.7 0.6 copy-start.5
  50.7 0.6 copy-start.6
  58.4 11.3 %all-to-all-start.1 = ((bf16[8,64,384]{2,1,0:T(8,128)(2,1)}), bf16[8,64,384]{2,1,0:T(8,128)(2,1)S(1)}, u32[]{:S(2)}, u32[]{:S(2)}) async-start(bf16[8,64,384]{2,1,0:T(8,128)(2,1)} %get-tuple-element.18), calls=%async_computation.1 | async-start | bytes 786432 | tf_op jit(solution)/shard_map/all_to_all | solution.py:18

commit v6 on v5

--- a/solution.py
+++ b/solution.py
@@ -142,16 +142,18 @@
     piece = unknowns // ways
     size = op_blocks.shape[2]
     deep = space // 2
-    along_z = [[h * deep + z * 2 + c for z in range(deep // 2)] for h in range(2) for c in range(2)]
+    ring = [*range(0, deep // 2, 2), *range(deep // 2 - 1, 0, -2)]
+    along_z = [[h * deep + z * 2 + c for z in ring] for h in range(2) for c in range(2)]
     across_z = [[h * deep + z * 2 + c for h in range(2) for c in range(2)] for z in range(deep // 2)]
     turns = [0, 3, 4, 7, 2, 1, 6, 5]
+    first_turns = [s ^ 1 for s in turns]
     around = [[p * ways + s for s in turns for p in group] for group in across_z]
     place = lax.axis_index("space").reshape(1).astype(jnp.int32)
 
-    coef_turned = jnp.concatenate([coef_primal[:, s * share : (s + 1) * share] for s in turns], axis=1)
+    coef_turned = jnp.concatenate([coef_primal[:, s * share : (s + 1) * share] for s in first_turns], axis=1)
     primal_part = jnp.einsum("mr,ms->rs", coef_turned, snaps_primal, preferred_element_type=F32)
     primal_tiles = primal_part.astype(BF16).reshape(ways, share, unknowns)
-    primal_tiles = exchange(primal_tiles, "snap", [turns])
+    primal_tiles = exchange(primal_tiles, "snap", [first_turns])
 
     adjoint_part = jnp.einsum("mr,ms->rs", coef_adjoint, snaps_adjoint, preferred_element_type=F32)
     adjoint_tiles = jnp.moveaxis(adjoint_part.astype(BF16).reshape(modes, ways, piece), 1, 0)

time: 124 us -> 123 us (level)
  waiting for transfers between devices: 27.5 us -> 21.5 us
  starting transfers between devices: 25.8 us -> 31.1 us
    all_to_all x3, waiting for transfers between devices: 26.6 us -> 20.6 us  [exchange(): lax.all_to_all(tiles, axis, 0, 0, tiled=True, axis_index_groups=groups)]
    all_to_all x3, starting transfers between devices: 13 us -> 17.2 us  [exchange(): lax.all_to_all(tiles, axis, 0, 0, tiled=True, axis_index_groups=groups)]
where the time goes in v6:
time: 123 us; the launch traced here: 122 us
  blocking collectives  51.1 us (42%)
  starting transfers between devices  31.1 us (25%)
  waiting for transfers between devices  21.5 us (17%)
  Pallas kernels  6.57 us (5%)
  matrix products  4.99 us (4%)
  local copies, waits for them, and re-layouts  4.93 us (4%)
    all_to_all x3, blocking collectives, exchange(): lax.all_to_all(tiles, axis, 0, 0, tiled=True, axis_index_groups=groups)  51.1 us
    all_to_all x3, waiting for transfers between devices, exchange(): lax.all_to_all(tiles, axis, 0, 0, tiled=True, axis_index_groups=groups)  20.6 us
    all_to_all x3, starting transfers between devices, exchange(): lax.all_to_all(tiles, axis, 0, 0, tiled=True, axis_index_groups=groups)  17.2 us
    ppermute x4, starting transfers between devices, swapped(): lax.ppermute(value, axis, [(a, b) for a, b in pairs] + [(b, a) for a, b i...  13.9 us
    pallas_call x1, Pallas kernels, applied_and_laid_out(): pl.pallas_call(apply_kernel, out_shape=[jax.ShapeDtypeStruct((share, unkn...  5.01 us
  transfers between devices with their start and end apart: 7, of which 4 were waited for; matrix products, arithmetic and copies ran while one was open for 3% of the time, Pallas kernels for 4%

profile of v6, /device:TPU:1, one launch (start us, length us, event | category | flops | bytes accessed | tf_op | source)
XLA Modules:
  0.0 122.0 jit_solution(17618474198894880965)
XLA Ops:
  0.6 1.1 fusion.2
  1.7 1.0 fusion.1
  3.0 1.7 %convolution_convert_fusion.1 = bf16[256,3072]{1,0:T(8,128)(2,1)} fusion(bf16[256,256]{1,0:T(8,128)(2,1)S(1)} %concatenate.4, bf16[256,3072]{1,0:T(8,128)(2,1)S(1)} %copy-done), kind=kOutput, calls=%fused_computation.1 | convolution fusion | flops 403439616 | bytes 3276800 | tf_op jit(solution)/shard_map/mr,ms->rs/dot_general | solution.py:154
  4.7 6.3 %all-to-all-start = ((bf16[8,32,3072]{2,1,0:T(8,128)(2,1)}), bf16[8,32,3072]{2,1,0:T(8,128)(2,1)S(1)}, u32[]{:S(2)}, u32[]{:S(2)}) async-start(bf16[8,32,3072]{2,1,0:T(8,128)(2,1)} %bitcast.28), calls=%async_computation | async-start | bytes 3145728 | tf_op jit(solution)/shard_map/all_to_all | solution.py:18
  11.0 2.0 %convolution_convert_fusion = bf16[256,3072]{1,0:T(8,128)(2,1)S(1)} fusion(bf16[256,256]{1,0:T(8,128)(2,1)S(1)} %copy-done.2, bf16[256,3072]{1,0:T(8,128)(2,1)} %param.9), kind=kOutput, calls=%fused_computation | convolution fusion | flops 403439616 | bytes 3276800 | tf_op jit(solution)/shard_map/mr,ms->rs/dot_general | solution.py:158
  13.0 1.3 %copy.16 = bf16[32,8,8,384]{3,2,0,1:T(8,128)(2,1)} copy(bf16[32,8,8,384]{3,2,1,0:T(8,128)(2,1)S(1)} %bitcast.29) | data formatting | bytes 3145728 | tf_op jit(solution)/shard_map/reshape | solution.py:159
  14.4 13.5 %all-to-all-done.tiles_ref = bf16[8,32,3072]{2,1,0:T(8,128)(2,1)S(1)} async-done(((bf16[8,32,3072]{2,1,0:T(8,128)(2,1)}), bf16[8,32,3072]{2,1,0:T(8,128)(2,1)S(1)}, u32[]{:S(2)}, u32[]{:S(2)}) %all-to-all-start) | async-done | bytes 1572896 | tf_op jit(solution)/shard_map/all_to_all | solution.py:18
  27.9 1.6 %shard_map.111 = (bf16[32,3072]{1,0:T(8,128)(2,1)}, bf16[6,32,128]{2,1,0:T(8,128)(2,1)S(1)}, bf16[6,32,128]{2,1,0:T(8,128)(2,1)S(1)}, bf16[6,32,128]{2,1,0:T(8,128)(2,1)S(1)}, bf16[6,32,128]{2,1,0:T(8,128)(2,1)S(1)}) custom-call(s32[1]{0:T(128)} %bitcast.place_ref, s32[4,6]{1,0:T(4,128)S(1)} %bitcast.26, bf16[8,32,3072]{2,1,0:T(8,128)(2,1)S(1)} %all-to-all-done.tiles_ref), custom_call_target="tpu_custom_call" | custom-call | tf_op jit(solution)/shard_map/pallas_call | solution.py:66
  29.4 5.6 %all-to-all-start.2 = ((bf16[8,256,384]{2,1,0:T(8,128)(2,1)}), bf16[8,256,384]{2,1,0:T(8,128)(2,1)S(1)}, u32[]{:S(2)}, u32[]{:S(2)}) async-start(bf16[8,256,384]{2,1,0:T(8,128)(2,1)} %bitcast.27), calls=%async_computation.2 | async-start | bytes 3145728 | tf_op jit(solution)/shard_map/all_to_all | solution.py:18
  35.1 0.7 collective-permute-start
  35.7 9.0 %collective-permute-start.1 = (bf16[6,32,128]{2,1,0:T(8,128)(2,1)S(1)}, bf16[6,32,128]{2,1,0:T(8,128)(2,1)S(1)}, u32[]{:S(2)}, u32[]{:S(2)}) collective-permute-start(bf16[6,32,128]{2,1,0:T(8,128)(2,1)S(1)} %get-tuple-element.14), channel_id=1, source_target_pairs={{8,16},{24,32},{40,48},{56,64},{72,80},{88,96},{104,112},{120,128}... | collective-permute-start | bytes 147464 | tf_op jit(solution)/shard_map/ppermute | solution.py:22
  44.7 1.9 %collective-permute-start.2 = (bf16[6,32,128]{2,1,0:T(8,128)(2,1)S(1)}, bf16[6,32,128]{2,1,0:T(8,128)(2,1)S(1)}, u32[]{:S(2)}, u32[]{:S(2)}) collective-permute-start(bf16[6,32,128]{2,1,0:T(8,128)(2,1)S(1)} %get-tuple-element.15), channel_id=1, source_target_pairs={{0,16},{8,24},{32,48},{40,56},{64,80},{72,88},{96,112},{104,120},{... | collective-permute-start | bytes 147464 | tf_op jit(solution)/shard_map/ppermute | solution.py:22
  46.7 2.3 %collective-permute-start.3 = (bf16[6,32,128]{2,1,0:T(8,128)(2,1)S(1)}, bf16[6,32,128]{2,1,0:T(8,128)(2,1)S(1)}, u32[]{:S(2)}, u32[]{:S(2)}) collective-permute-start(bf16[6,32,128]{2,1,0:T(8,128)(2,1)S(1)} %get-tuple-element.16), channel_id=1, source_target_pairs={{0,8},{16,24},{32,40},{48,56},{64,72},{80,88},{96,104},{112,120},{... | collective-permute-start | bytes 147464 | tf_op jit(solution)/shard_map/ppermute | solution.py:22
  49.0 0.8 collective-permute-done.2.refs_2_
  49.9 0.6 copy-done.5
  50.5 5.0 %shard_map.112 = (bf16[32,3072]{1,0:T(8,128)(2,1)}, bf16[8,64,384]{2,1,0:T(8,128)(2,1)}) custom-call(s32[1]{0:T(128)} %bitcast.place_ref, s32[24]{0:T(128)} %counts_ref.1, s32[5,24]{1,0:T(8,128)} %bitcast.33, bf16[32,3072]{1,0:T(8,128)(2,1)} %get-tuple-element.8.primal_ref, bf16[6,32,128]{2,1,0:T(8,128)(2,1)} %copy-done.3, bf16[6,32,128]{2,1,0:T(8,128)(2,1)} %copy-done.4, ...), custom_call_target="tpu_custom_call" | custom-call | tf_op jit(solution)/shard_map/pallas_call | solution.py:116
  55.6 5.3 %all-to-all-start.1 = ((bf16[8,64,384]{2,1,0:T(8,128)(2,1)}), bf16[8,64,384]{2,1,0:T(8,128)(2,1)S(1)}, u32[]{:S(2)}, u32[]{:S(2)}) async-start(bf16[8,64,384]{2,1,0:T(8,128)(2,1)} %get-tuple-element.18), calls=%async_computation.1 | async-start | bytes 786432 | tf_op jit(solution)/shard_map/all_to_all | solution.py:18
  61.0 0.9 reduce_sum.33
  61.9 7.0 %all-to-all-done.1 = bf16[8,64,384]{2,1,0:T(8,128)(2,1)S(1)} async-done(((bf16[8,64,384]{2,1,0:T(8,128)(2,1)}), bf16[8,64,384]{2,1,0:T(8,128)(2,1)S(1)}, u32[]{:S(2)}, u32[]{:S(2)}) %all-to-all-start.1) | async-done | bytes 393248 | tf_op jit(solution)/shard_map/all_to_all | solution.py:18
  68.9 1.2 %convolution_convert_fusion.2 = bf16[8,64,256]{2,1,0:T(8,128)(2,1)S(1)} fusion(bf16[8,64,384]{2,1,0:T(8,128)(2,1)S(1)} %all-to-all-done.1, bf16[256,384]{1,0:T(8,128)(2,1)} %reduce_sum.33), kind=kOutput, calls=%fused_computation.3 | convolution fusion | flops 100794368 | bytes 851968 | tf_op jit(solution)/shard_map/was,bs->wab/dot_general | solution.py:169
  70.2 22.5 %all_to_all.30 = bf16[32,16,256]{2,1,0:T(8,128)(2,1)S(1)} all-to-all(bf16[32,16,256]{2,1,0:T(8,128)(2,1)S(1)} %bitcast.30), channel_id=1, replica_groups={{0,8,256,264,3,11,259,267,4,12,260,268,7,15,263,271,2,10,258,266,1,9,25..., dimensions={0} | all-to-all | bytes 524288 | tf_op jit(solution)/shard_map/all_to_all | solution.py:18
  92.7 18.9 %all_to_all.31 = bf16[16,16,256]{2,1,0:T(8,128)(2,1)S(1)} all-to-all(bf16[16,16,256]{2,1,0:T(8,128)(2,1)S(1)} %broadcast_in_dim.4), channel_id=1, replica_groups={{0,32,64,96,128,160,192,224,240,208,176,144,112,80,48,16},{8,40,72,104,..., dimensions={0} | all-to-all | bytes 262144 | tf_op jit(solution)/shard_map/all_to_all | solution.py:18
  111.6 9.7 %all_to_all.32 = f32[4,16,256]{2,1,0:T(8,128)S(1)} all-to-all(f32[4,16,256]{2,1,0:T(8,128)S(1)} %broadcast_in_dim.5), channel_id=1, replica_groups={{0,8,256,264},{16,24,272,280},{32,40,288,296},{48,56,304,312},{64,72,32..., dimensions={0} | all-to-all | bytes 131072 | tf_op jit(solution)/shard_map/all_to_all | solution.py:18
  121.4 0.6 fusion.3
  (23 shorter events, 0.4 us)
Async XLA Ops:
  0.6 2.3 %copy-start = (bf16[256,3072]{1,0:T(8,128)(2,1)S(1)}, bf16[256,3072]{1,0:T(8,128)(2,1)}, u32[]{:S(2)}) copy-start(bf16[256,3072]{1,0:T(8,128)(2,1)} %param.8) | copy-start | bytes 4718596
  4.7 6.3 %copy-start.2 = (bf16[256,256]{1,0:T(8,128)(2,1)S(1)}, bf16[256,256]{1,0:T(8,128)(2,1)}, u32[]{:S(2)}) copy-start(bf16[256,256]{1,0:T(8,128)(2,1)} %param.11) | copy-start | bytes 393220
  4.7 23.1 %all-to-all-start = ((bf16[8,32,3072]{2,1,0:T(8,128)(2,1)}), bf16[8,32,3072]{2,1,0:T(8,128)(2,1)S(1)}, u32[]{:S(2)}, u32[]{:S(2)}) async-start(bf16[8,32,3072]{2,1,0:T(8,128)(2,1)} %bitcast.28), calls=%async_computation | async-start | bytes 3145728 | tf_op jit(solution)/shard_map/all_to_all | solution.py:18
  13.0 14.9 %copy-start.1 = (s32[1,4,6]{2,1,0:T(4,128)S(1)}, s32[1,4,6]{2,1,0:T(4,128)}, u32[]{:S(2)}) copy-start(s32[1,4,6]{2,1,0:T(4,128)} %param.15) | copy-start | bytes 292
  29.4 26.2 %all-to-all-start.2 = ((bf16[8,256,384]{2,1,0:T(8,128)(2,1)}), bf16[8,256,384]{2,1,0:T(8,128)(2,1)S(1)}, u32[]{:S(2)}, u32[]{:S(2)}) async-start(bf16[8,256,384]{2,1,0:T(8,128)(2,1)} %bitcast.27), calls=%async_computation.2 | async-start | bytes 3145728 | tf_op jit(solution)/shard_map/all_to_all | solution.py:18
  35.1 13.9 %collective-permute-start = (bf16[6,32,128]{2,1,0:T(8,128)(2,1)S(1)}, bf16[6,32,128]{2,1,0:T(8,128)(2,1)S(1)}, u32[]{:S(2)}, u32[]{:S(2)}) collective-permute-start(bf16[6,32,128]{2,1,0:T(8,128)(2,1)S(1)} %get-tuple-element.13), channel_id=1, source_target_pairs={{16,32},{24,40},{48,64},{56,72},{80,96},{88,104},{112,128},{120,13... | collective-permute-start | bytes 147464 | tf_op jit(solution)/shard_map/ppermute | solution.py:22
  35.7 13.3 %collective-permute-start.1 = (bf16[6,32,128]{2,1,0:T(8,128)(2,1)S(1)}, bf16[6,32,128]{2,1,0:T(8,128)(2,1)S(1)}, u32[]{:S(2)}, u32[]{:S(2)}) collective-permute-start(bf16[6,32,128]{2,1,0:T(8,128)(2,1)S(1)} %get-tuple-element.14), channel_id=1, source_target_pairs={{8,16},{24,32},{40,48},{56,64},{72,80},{88,96},{104,112},{120,128}... | collective-permute-start | bytes 147464 | tf_op jit(solution)/shard_map/ppermute | solution.py:22
  44.7 5.1 %collective-permute-start.2 = (bf16[6,32,128]{2,1,0:T(8,128)(2,1)S(1)}, bf16[6,32,128]{2,1,0:T(8,128)(2,1)S(1)}, u32[]{:S(2)}, u32[]{:S(2)}) collective-permute-start(bf16[6,32,128]{2,1,0:T(8,128)(2,1)S(1)} %get-tuple-element.15), channel_id=1, source_target_pairs={{0,16},{8,24},{32,48},{40,56},{64,80},{72,88},{96,112},{104,120},{... | collective-permute-start | bytes 147464 | tf_op jit(solution)/shard_map/ppermute | solution.py:22
  46.7 3.2 %collective-permute-start.3 = (bf16[6,32,128]{2,1,0:T(8,128)(2,1)S(1)}, bf16[6,32,128]{2,1,0:T(8,128)(2,1)S(1)}, u32[]{:S(2)}, u32[]{:S(2)}) collective-permute-start(bf16[6,32,128]{2,1,0:T(8,128)(2,1)S(1)} %get-tuple-element.16), channel_id=1, source_target_pairs={{0,8},{16,24},{32,40},{48,56},{64,72},{80,88},{96,104},{112,120},{... | collective-permute-start | bytes 147464 | tf_op jit(solution)/shard_map/ppermute | solution.py:22
  49.0 0.9 copy-start.3
  49.0 0.9 copy-start.4
  49.9 0.6 copy-start.5
  49.9 0.6 copy-start.6
  55.6 13.3 %all-to-all-start.1 = ((bf16[8,64,384]{2,1,0:T(8,128)(2,1)}), bf16[8,64,384]{2,1,0:T(8,128)(2,1)S(1)}, u32[]{:S(2)}, u32[]{:S(2)}) async-start(bf16[8,64,384]{2,1,0:T(8,128)(2,1)} %get-tuple-element.18), calls=%async_computation.1 | async-start | bytes 786432 | tf_op jit(solution)/shard_map/all_to_all | solution.py:18

commit v7 on v6

--- a/solution.py
+++ b/solution.py
@@ -145,8 +145,8 @@
     ring = [*range(0, deep // 2, 2), *range(deep // 2 - 1, 0, -2)]
     along_z = [[h * deep + z * 2 + c for z in ring] for h in range(2) for c in range(2)]
     across_z = [[h * deep + z * 2 + c for h in range(2) for c in range(2)] for z in range(deep // 2)]
-    turns = [0, 3, 4, 7, 2, 1, 6, 5]
-    first_turns = [s ^ 1 for s in turns]
+    turns = [3, 4, 7, 2, 1, 6, 5, 0]
+    first_turns = [1, 2, 5, 6, 3, 0, 7, 4]
     around = [[p * ways + s for s in turns for p in group] for group in across_z]
     place = lax.axis_index("space").reshape(1).astype(jnp.int32)
 

time: 123 us -> 122 us (level)
  transfers between devices with their start and end apart: 7 -> 7, of which waited for: 4 -> 3; matrix products, arithmetic and copies ran while one was open for 3% -> 3% of each run, Pallas kernels for 4% -> 4%
where the time goes in v7:
time: 122 us
  blocking collectives  50.5 us (41%)
  starting transfers between devices  31.8 us (26%)
  waiting for transfers between devices  21.1 us (17%)
  Pallas kernels  6.58 us (5%)
  matrix products  4.99 us (4%)
  local copies, waits for them, and re-layouts  4.93 us (4%)
    all_to_all x3, blocking collectives, exchange(): lax.all_to_all(tiles, axis, 0, 0, tiled=True, axis_index_groups=groups)  50.5 us
    all_to_all x3, waiting for transfers between devices, exchange(): lax.all_to_all(tiles, axis, 0, 0, tiled=True, axis_index_groups=groups)  20.3 us
    all_to_all x3, starting transfers between devices, exchange(): lax.all_to_all(tiles, axis, 0, 0, tiled=True, axis_index_groups=groups)  18.2 us
    ppermute x4, starting transfers between devices, swapped(): lax.ppermute(value, axis, [(a, b) for a, b in pairs] + [(b, a) for a, b i...  13.6 us
    pallas_call x1, Pallas kernels, applied_and_laid_out(): pl.pallas_call(apply_kernel, out_shape=[jax.ShapeDtypeStruct((share, unkn...  5.02 us
  transfers between devices with their start and end apart: 7, of which 3 were waited for; matrix products, arithmetic and copies ran while one was open for 3% of the time, Pallas kernels for 4%

profile of v7, /device:TPU:1, one launch (start us, length us, event | category | flops | bytes accessed | tf_op | source)
XLA Modules:
  0.0 121.7 jit_solution(1405623977840915067)
XLA Ops:
  0.6 1.1 fusion.2
  1.7 1.0 fusion.1
  3.0 1.7 %convolution_convert_fusion.1 = bf16[256,3072]{1,0:T(8,128)(2,1)} fusion(bf16[256,256]{1,0:T(8,128)(2,1)S(1)} %concatenate.4, bf16[256,3072]{1,0:T(8,128)(2,1)S(1)} %copy-done), kind=kOutput, calls=%fused_computation.1 | convolution fusion | flops 403439616 | bytes 3276800 | tf_op jit(solution)/shard_map/mr,ms->rs/dot_general | solution.py:154
  4.7 6.3 %all-to-all-start = ((bf16[8,32,3072]{2,1,0:T(8,128)(2,1)}), bf16[8,32,3072]{2,1,0:T(8,128)(2,1)S(1)}, u32[]{:S(2)}, u32[]{:S(2)}) async-start(bf16[8,32,3072]{2,1,0:T(8,128)(2,1)} %bitcast.28), calls=%async_computation | async-start | bytes 3145728 | tf_op jit(solution)/shard_map/all_to_all | solution.py:18
  11.0 2.0 %convolution_convert_fusion = bf16[256,3072]{1,0:T(8,128)(2,1)S(1)} fusion(bf16[256,256]{1,0:T(8,128)(2,1)S(1)} %copy-done.2, bf16[256,3072]{1,0:T(8,128)(2,1)} %param.9), kind=kOutput, calls=%fused_computation | convolution fusion | flops 403439616 | bytes 3276800 | tf_op jit(solution)/shard_map/mr,ms->rs/dot_general | solution.py:158
  13.0 1.3 %copy.16 = bf16[32,8,8,384]{3,2,0,1:T(8,128)(2,1)} copy(bf16[32,8,8,384]{3,2,1,0:T(8,128)(2,1)S(1)} %bitcast.29) | data formatting | bytes 3145728 | tf_op jit(solution)/shard_map/reshape | solution.py:159
  14.4 13.5 %all-to-all-done.tiles_ref = bf16[8,32,3072]{2,1,0:T(8,128)(2,1)S(1)} async-done(((bf16[8,32,3072]{2,1,0:T(8,128)(2,1)}), bf16[8,32,3072]{2,1,0:T(8,128)(2,1)S(1)}, u32[]{:S(2)}, u32[]{:S(2)}) %all-to-all-start) | async-done | bytes 1572896 | tf_op jit(solution)/shard_map/all_to_all | solution.py:18
  27.9 1.6 %shard_map.111 = (bf16[32,3072]{1,0:T(8,128)(2,1)}, bf16[6,32,128]{2,1,0:T(8,128)(2,1)S(1)}, bf16[6,32,128]{2,1,0:T(8,128)(2,1)S(1)}, bf16[6,32,128]{2,1,0:T(8,128)(2,1)S(1)}, bf16[6,32,128]{2,1,0:T(8,128)(2,1)S(1)}) custom-call(s32[1]{0:T(128)} %bitcast.place_ref, s32[4,6]{1,0:T(4,128)S(1)} %bitcast.26, bf16[8,32,3072]{2,1,0:T(8,128)(2,1)S(1)} %all-to-all-done.tiles_ref), custom_call_target="tpu_custom_call" | custom-call | tf_op jit(solution)/shard_map/pallas_call | solution.py:66
  29.4 6.8 %all-to-all-start.2 = ((bf16[8,256,384]{2,1,0:T(8,128)(2,1)}), bf16[8,256,384]{2,1,0:T(8,128)(2,1)S(1)}, u32[]{:S(2)}, u32[]{:S(2)}) async-start(bf16[8,256,384]{2,1,0:T(8,128)(2,1)} %bitcast.27), calls=%async_computation.2 | async-start | bytes 3145728 | tf_op jit(solution)/shard_map/all_to_all | solution.py:18
  36.2 0.7 collective-permute-start
  36.9 8.7 %collective-permute-start.1 = (bf16[6,32,128]{2,1,0:T(8,128)(2,1)S(1)}, bf16[6,32,128]{2,1,0:T(8,128)(2,1)S(1)}, u32[]{:S(2)}, u32[]{:S(2)}) collective-permute-start(bf16[6,32,128]{2,1,0:T(8,128)(2,1)S(1)} %get-tuple-element.14), channel_id=1, source_target_pairs={{8,16},{24,32},{40,48},{56,64},{72,80},{88,96},{104,112},{120,128}... | collective-permute-start | bytes 147464 | tf_op jit(solution)/shard_map/ppermute | solution.py:22
  45.6 1.9 %collective-permute-start.2 = (bf16[6,32,128]{2,1,0:T(8,128)(2,1)S(1)}, bf16[6,32,128]{2,1,0:T(8,128)(2,1)S(1)}, u32[]{:S(2)}, u32[]{:S(2)}) collective-permute-start(bf16[6,32,128]{2,1,0:T(8,128)(2,1)S(1)} %get-tuple-element.15), channel_id=1, source_target_pairs={{0,16},{8,24},{32,48},{40,56},{64,80},{72,88},{96,112},{104,120},{... | collective-permute-start | bytes 147464 | tf_op jit(solution)/shard_map/ppermute | solution.py:22
  47.5 2.3 %collective-permute-start.3 = (bf16[6,32,128]{2,1,0:T(8,128)(2,1)S(1)}, bf16[6,32,128]{2,1,0:T(8,128)(2,1)S(1)}, u32[]{:S(2)}, u32[]{:S(2)}) collective-permute-start(bf16[6,32,128]{2,1,0:T(8,128)(2,1)S(1)} %get-tuple-element.16), channel_id=1, source_target_pairs={{0,8},{16,24},{32,40},{48,56},{64,72},{80,88},{96,104},{112,120},{... | collective-permute-start | bytes 147464 | tf_op jit(solution)/shard_map/ppermute | solution.py:22
  49.9 0.8 collective-permute-done.2.refs_2_
  50.8 0.6 copy-done.5
  51.4 5.0 %shard_map.112 = (bf16[32,3072]{1,0:T(8,128)(2,1)}, bf16[8,64,384]{2,1,0:T(8,128)(2,1)}) custom-call(s32[1]{0:T(128)} %bitcast.place_ref, s32[24]{0:T(128)} %counts_ref.1, s32[5,24]{1,0:T(8,128)} %bitcast.33, bf16[32,3072]{1,0:T(8,128)(2,1)} %get-tuple-element.8.primal_ref, bf16[6,32,128]{2,1,0:T(8,128)(2,1)} %copy-done.3, bf16[6,32,128]{2,1,0:T(8,128)(2,1)} %copy-done.4, ...), custom_call_target="tpu_custom_call" | custom-call | tf_op jit(solution)/shard_map/pallas_call | solution.py:116
  56.4 5.1 %all-to-all-start.1 = ((bf16[8,64,384]{2,1,0:T(8,128)(2,1)}), bf16[8,64,384]{2,1,0:T(8,128)(2,1)S(1)}, u32[]{:S(2)}, u32[]{:S(2)}) async-start(bf16[8,64,384]{2,1,0:T(8,128)(2,1)} %get-tuple-element.18), calls=%async_computation.1 | async-start | bytes 786432 | tf_op jit(solution)/shard_map/all_to_all | solution.py:18
  61.5 0.9 reduce_sum.33
  62.5 6.7 %all-to-all-done.1 = bf16[8,64,384]{2,1,0:T(8,128)(2,1)S(1)} async-done(((bf16[8,64,384]{2,1,0:T(8,128)(2,1)}), bf16[8,64,384]{2,1,0:T(8,128)(2,1)S(1)}, u32[]{:S(2)}, u32[]{:S(2)}) %all-to-all-start.1) | async-done | bytes 393248 | tf_op jit(solution)/shard_map/all_to_all | solution.py:18
  69.2 1.2 %convolution_convert_fusion.2 = bf16[8,64,256]{2,1,0:T(8,128)(2,1)S(1)} fusion(bf16[8,64,384]{2,1,0:T(8,128)(2,1)S(1)} %all-to-all-done.1, bf16[256,384]{1,0:T(8,128)(2,1)} %reduce_sum.33), kind=kOutput, calls=%fused_computation.3 | convolution fusion | flops 100794368 | bytes 851968 | tf_op jit(solution)/shard_map/was,bs->wab/dot_general | solution.py:169
  70.5 20.2 %all_to_all.30 = bf16[32,16,256]{2,1,0:T(8,128)(2,1)S(1)} all-to-all(bf16[32,16,256]{2,1,0:T(8,128)(2,1)S(1)} %bitcast.30), channel_id=1, replica_groups={{3,11,259,267,4,12,260,268,7,15,263,271,2,10,258,266,1,9,257,265,6,14,2..., dimensions={0} | all-to-all | bytes 524288 | tf_op jit(solution)/shard_map/all_to_all | solution.py:18
  90.7 20.0 %all_to_all.31 = bf16[16,16,256]{2,1,0:T(8,128)(2,1)S(1)} all-to-all(bf16[16,16,256]{2,1,0:T(8,128)(2,1)S(1)} %broadcast_in_dim.4), channel_id=1, replica_groups={{0,32,64,96,128,160,192,224,240,208,176,144,112,80,48,16},{8,40,72,104,..., dimensions={0} | all-to-all | bytes 262144 | tf_op jit(solution)/shard_map/all_to_all | solution.py:18
  110.7 10.3 %all_to_all.32 = f32[4,16,256]{2,1,0:T(8,128)S(1)} all-to-all(f32[4,16,256]{2,1,0:T(8,128)S(1)} %broadcast_in_dim.5), channel_id=1, replica_groups={{0,8,256,264},{16,24,272,280},{32,40,288,296},{48,56,304,312},{64,72,32..., dimensions={0} | all-to-all | bytes 131072 | tf_op jit(solution)/shard_map/all_to_all | solution.py:18
  121.1 0.6 fusion.3
  (23 shorter events, 0.3 us)
Async XLA Ops:
  0.6 2.3 %copy-start = (bf16[256,3072]{1,0:T(8,128)(2,1)S(1)}, bf16[256,3072]{1,0:T(8,128)(2,1)}, u32[]{:S(2)}) copy-start(bf16[256,3072]{1,0:T(8,128)(2,1)} %param.8) | copy-start | bytes 4718596
  4.7 6.3 %copy-start.2 = (bf16[256,256]{1,0:T(8,128)(2,1)S(1)}, bf16[256,256]{1,0:T(8,128)(2,1)}, u32[]{:S(2)}) copy-start(bf16[256,256]{1,0:T(8,128)(2,1)} %param.11) | copy-start | bytes 393220
  4.7 23.1 %all-to-all-start = ((bf16[8,32,3072]{2,1,0:T(8,128)(2,1)}), bf16[8,32,3072]{2,1,0:T(8,128)(2,1)S(1)}, u32[]{:S(2)}, u32[]{:S(2)}) async-start(bf16[8,32,3072]{2,1,0:T(8,128)(2,1)} %bitcast.28), calls=%async_computation | async-start | bytes 3145728 | tf_op jit(solution)/shard_map/all_to_all | solution.py:18
  13.0 14.9 %copy-start.1 = (s32[1,4,6]{2,1,0:T(4,128)S(1)}, s32[1,4,6]{2,1,0:T(4,128)}, u32[]{:S(2)}) copy-start(s32[1,4,6]{2,1,0:T(4,128)} %param.15) | copy-start | bytes 292
  29.4 27.0 %all-to-all-start.2 = ((bf16[8,256,384]{2,1,0:T(8,128)(2,1)}), bf16[8,256,384]{2,1,0:T(8,128)(2,1)S(1)}, u32[]{:S(2)}, u32[]{:S(2)}) async-start(bf16[8,256,384]{2,1,0:T(8,128)(2,1)} %bitcast.27), calls=%async_computation.2 | async-start | bytes 3145728 | tf_op jit(solution)/shard_map/all_to_all | solution.py:18
  36.2 13.6 %collective-permute-start = (bf16[6,32,128]{2,1,0:T(8,128)(2,1)S(1)}, bf16[6,32,128]{2,1,0:T(8,128)(2,1)S(1)}, u32[]{:S(2)}, u32[]{:S(2)}) collective-permute-start(bf16[6,32,128]{2,1,0:T(8,128)(2,1)S(1)} %get-tuple-element.13), channel_id=1, source_target_pairs={{16,32},{24,40},{48,64},{56,72},{80,96},{88,104},{112,128},{120,13... | collective-permute-start | bytes 147464 | tf_op jit(solution)/shard_map/ppermute | solution.py:22
  36.9 13.0 %collective-permute-start.1 = (bf16[6,32,128]{2,1,0:T(8,128)(2,1)S(1)}, bf16[6,32,128]{2,1,0:T(8,128)(2,1)S(1)}, u32[]{:S(2)}, u32[]{:S(2)}) collective-permute-start(bf16[6,32,128]{2,1,0:T(8,128)(2,1)S(1)} %get-tuple-element.14), channel_id=1, source_target_pairs={{8,16},{24,32},{40,48},{56,64},{72,80},{88,96},{104,112},{120,128}... | collective-permute-start | bytes 147464 | tf_op jit(solution)/shard_map/ppermute | solution.py:22
  45.6 5.1 %collective-permute-start.2 = (bf16[6,32,128]{2,1,0:T(8,128)(2,1)S(1)}, bf16[6,32,128]{2,1,0:T(8,128)(2,1)S(1)}, u32[]{:S(2)}, u32[]{:S(2)}) collective-permute-start(bf16[6,32,128]{2,1,0:T(8,128)(2,1)S(1)} %get-tuple-element.15), channel_id=1, source_target_pairs={{0,16},{8,24},{32,48},{40,56},{64,80},{72,88},{96,112},{104,120},{... | collective-permute-start | bytes 147464 | tf_op jit(solution)/shard_map/ppermute | solution.py:22
  47.5 3.2 %collective-permute-start.3 = (bf16[6,32,128]{2,1,0:T(8,128)(2,1)S(1)}, bf16[6,32,128]{2,1,0:T(8,128)(2,1)S(1)}, u32[]{:S(2)}, u32[]{:S(2)}) collective-permute-start(bf16[6,32,128]{2,1,0:T(8,128)(2,1)S(1)} %get-tuple-element.16), channel_id=1, source_target_pairs={{0,8},{16,24},{32,40},{48,56},{64,72},{80,88},{96,104},{112,120},{... | collective-permute-start | bytes 147464 | tf_op jit(solution)/shard_map/ppermute | solution.py:22
  49.8 0.9 copy-start.3
  49.9 0.9 copy-start.4
  50.7 0.6 copy-start.5
  50.7 0.6 copy-start.6
  56.4 12.8 %all-to-all-start.1 = ((bf16[8,64,384]{2,1,0:T(8,128)(2,1)}), bf16[8,64,384]{2,1,0:T(8,128)(2,1)S(1)}, u32[]{:S(2)}, u32[]{:S(2)}) async-start(bf16[8,64,384]{2,1,0:T(8,128)(2,1)} %get-tuple-element.18), calls=%async_computation.1 | async-start | bytes 786432 | tf_op jit(solution)/shard_map/all_to_all | solution.py:18
